TPU v7x, 512 devices: a whole 4x8x8 slice. The times are simulated.
512 devices in a mesh: dp: 64 (over z_lo, y, core), expert: 8 (over x, z_hi).
Axes of the slice: x: 4, y: 8, z: 8 (z_hi: 2, z_lo: 4; z = z_hi * 4 + z_lo), core: 2. Of those that a mesh axis runs over, the one named last changes fastest.
Arguments:
- tokens: bfloat16 [131072, 1024], P(('dp', 'expert')), may hold values from -6 to 6
- expert_ids: int32 [131072], P(('dp', 'expert')), may hold values from 0 to 7
- slots: int32 [131072], P(('dp', 'expert')), may hold values from -1 to 39, as said below
- router: bfloat16 [1024, 8], replicated, may hold values from -0.1875 to 0.1875
- w_in: bfloat16 [8, 1024, 2048], P('expert', 'dp'), may hold values from -0.1875 to 0.1875
- w_out: bfloat16 [8, 2048, 1024], P('expert', None, 'dp'), may hold values from -0.125 to 0.125
- texts: bfloat16 [2048, 1024], P(('dp', 'expert')), may hold values from -6 to 6
Outputs:
- d_tokens: bfloat16 [131072, 1024], P(('dp', 'expert'))
- d_texts: float32 [2048, 1024], P(('dp', 'expert'))
- router_grad: float32 [1024, 8], replicated
Inputs may be any that keep to these rules, and one draw needn't show every extreme that they name: Within each block of 256 tokens (one device's), the tokens of each expert hold slots 0, 1, 2, ... in token order until 40, and -1 after. On every index of dp, some expert receives all 40 slots from each of the 8 blocks of that index.
All inputs are finite; a program needn't handle non-finite values.
Results may differ from a plain program's by a relative error of at most 0.0064.
Values may be sent and summed in bfloat16 or wider, within the bound.
No kernel may reach another device: no remote copies, remote signals or barrier semaphores. Data moves between devices by JAX's collectives and lax.ppermute only.
A program may use at most 64 MiB of HBM per device.

v0:
```python
import functools

import jax
import jax.numpy as jnp
from jax import lax
from jax.experimental import pallas as pl
from jax.experimental.pallas import tpu as pltpu
from jax.sharding import Mesh
from jax.sharding import PartitionSpec as P


highest = lax.Precision.HIGHEST
temper = 10.0
offset = -2.0
loss_scale = 256.0
epsilon = 1e-06

AXES = ("a", "b", "y", "c", "x", "zh")
DP = ("a", "b", "y", "c")
GROUP = ("x", "b")
OWNERS = ("a", "y", "c", "zh")
DEEP = ("a", "b", "c", "zh")

ANY = pl.BlockSpec(memory_space=pl.ANY)
VMEM = pl.BlockSpec(memory_space=pltpu.VMEM)
SMEM = pl.BlockSpec(memory_space=pltpu.SMEM)


def deep_index(z, core):
    return ((z // 2) % 2 * 2 + z % 2) * 4 + core * 2 + z // 4


def depth_round(n):
    route = []
    for core in range(2):
        for p in range(2):
            for i in range(4):
                start, end = 4 * p + i, 2 * ((i + 2 * core + n) % 4) + p
                route.append((deep_index(start, core), deep_index(end, core)))
    return route


def ring_route():
    up = [(2 * y, 2 * ((y + 1) % 8)) for y in range(8)]
    down = [(2 * y + 1, 2 * ((y - 1) % 8) + 1) for y in range(8)]
    return up + down


def swap_cores(block):
    return lax.ppermute(block, "c", [(0, 1), (1, 0)])


def contract_last(left, right):
    return lax.dot_general(
        left, right, (((1,), (1,)), ((), ())), preferred_element_type=jnp.float32
    )


def start_copies(where, parts, refs, w_ref, sem, kind):
    y, j, c = where[0], where[1], where[2]
    for ref, (step, swapped, flip) in zip(refs, parts):
        ahead = 2 * c - 1 if not swapped else 1 - 2 * c
        at_y = lax.rem(y + 8 + ahead * step, 8)
        holder = 1 - c if flip else c
        for lead in range(4):
            core = holder if lead % 2 == 0 else 1 - holder
            at_zl = lax.rem(j + 4 - (2 * holder + lead // 2), 4)
            row = pl.multiple_of(((at_zl * 8 + at_y) * 2 + core) * 16, 16)
            src = ref.at[lead, pl.ds(kind * 16, 16), :]
            pltpu.make_async_copy(src, w_ref.at[pl.ds(row, 16), :], sem).start()


def wait_all(w_ref, sem):
    pltpu.make_async_copy(w_ref, w_ref, sem).wait()


def forward_kernel(parts, count, where, x_ref, mix_ref, *rest):
    refs, (hid_ref, out_ref, part_ref, win, wout, act, sems) = rest[:count], rest[count:]
    start_copies(where, parts, refs, win, sems.at[0], 0)
    start_copies(where, parts, refs, wout, sems.at[1], 1)
    wait_all(win, sems.at[0])
    for n in range(4):
        at = slice(n * 512, n * 512 + 512)
        hidden = jnp.dot(x_ref[...], win[:, at], preferred_element_type=jnp.float32)
        hid_ref[:, at] = hidden
        act[:, at] = jax.nn.gelu(hidden, approximate=True).astype(jnp.bfloat16)
    wait_all(wout, sems.at[1])
    for n in range(4):
        at = slice(n * 256, n * 256 + 256)
        out = contract_last(act[...], wout[at, :]).astype(jnp.bfloat16)
        out_ref[:, at] = out
        part = jnp.dot(
            mix_ref[...],
            out.astype(jnp.float32),
            precision=highest,
            preferred_element_type=jnp.float32,
        ).astype(jnp.bfloat16)
        for member in range(part_ref.shape[0]):
            part_ref[member, :, at] = part


def gelu_slope(hidden):
    scale = 0.7978845608028654
    square = hidden * hidden
    bent = jnp.tanh(scale * (hidden + 0.044715 * (square * hidden)))
    inner = scale * (1.0 + 3.0 * 0.044715 * square)
    return 0.5 * (1.0 + bent) + 0.5 * hidden * (1.0 - bent * bent) * inner


def backward_kernel(parts, count, where, dy_ref, hid_ref, grad_logit, router_row, *rest):
    refs, (back_ref, win, wout, dhid, sems) = rest[:count], rest[count:]
    start_copies(where, parts, refs, wout, sems.at[1], 1)
    start_copies(where, parts, refs, win, sems.at[0], 0)
    wait_all(wout, sems.at[1])
    for n in range(4):
        at = slice(n * 512, n * 512 + 512)
        grad = jnp.dot(dy_ref[...], wout[:, at], preferred_element_type=jnp.float32)
        dhid[:, at] = (grad * gelu_slope(hid_ref[:, at])).astype(jnp.bfloat16)
    wait_all(win, sems.at[0])
    members, _, width = back_ref.shape
    capacity = dhid.shape[0] // members
    back_ref[:, capacity:, :] = jnp.zeros((members, 8, width), jnp.bfloat16)
    for n in range(4):
        at = slice(n * 256, n * 256 + 256)
        moved = contract_last(dhid[...], win[at, :]).astype(jnp.bfloat16)
        rows = moved.astype(jnp.float32) + grad_logit[...] * router_row[:, at]
        for member in range(members):
            block = rows[member * capacity : (member + 1) * capacity]
            back_ref[member, :capacity, at] = block.astype(jnp.bfloat16)


def gathered_weights(w_in, w_out, settle):
    own = jnp.concatenate([w_in[0], w_out[0].T], axis=0)
    pair = jnp.stack([own, swap_cores(own)])
    mine = jnp.concatenate([lax.ppermute(pair, DEEP, depth_round(n)) for n in range(2)])
    theirs = swap_cores(mine)
    arrays, parts = [mine, theirs], [(0, False, False), (0, False, True)]
    chunks = [mine, theirs]
    for step in range(1, 5):
        for n in range(2 if step < 4 else 1):
            moved = lax.ppermute(chunks[n], ("y", "c"), ring_route())
            chunks[n] = moved
            arrays.append(moved)
            parts.append((step, False, n == 1))
            if step == 4:
                moved, settled = lax.optimization_barrier((moved, settle()))
            arrays.append(swap_cores(moved))
            parts.append((step, True, n == 0))
    return arrays, parts, settled


def share(block, axes, count):
    return lax.all_to_all(
        jnp.broadcast_to(block[None], (count,) + block.shape), axes, 0, 0, tiled=True
    )


def unit_rows(matrix):
    scales = lax.rsqrt(jnp.sum(matrix * matrix, axis=1, keepdims=True) + epsilon)
    return matrix * scales, scales


def layer(tokens, expert_ids, slots, router, w_in, w_out, texts):
    tok_count, width = tokens.shape
    experts = router.shape[1]
    capacity = 5 * tok_count // (4 * experts)
    images = texts.shape[0]
    patch = tok_count // images
    slot_total = experts * capacity
    rows = slot_total
    hidden_width = w_in.shape[2]
    f32, bf16 = jnp.float32, jnp.bfloat16
    me = lax.axis_index(GROUP)
    pictures = experts * images

    before = lax.ppermute(texts, DP, [(i, (i + 1) % 64) for i in range(64)])
    places = jnp.where(slots >= 0, expert_ids * capacity + slots, slot_total)
    picks = (jnp.arange(slot_total, dtype=jnp.int32)[:, None] == places[None, :]).astype(bf16)
    image_of = me * images + jnp.arange(tok_count, dtype=jnp.int32) // patch
    marks = (image_of[:, None] == jnp.arange(128, dtype=jnp.int32)[None, :]).astype(bf16)
    wide = jnp.concatenate([tokens, marks], axis=1)
    send = jnp.dot(picks, wide, preferred_element_type=f32).astype(bf16)
    pair = jnp.pad(jnp.concatenate([texts, before], axis=0), ((0, 0), (0, 128)))
    send = jnp.concatenate(
        [
            send.reshape(experts, capacity, width + 128),
            jnp.broadcast_to(pair[None], (experts,) + pair.shape),
        ],
        axis=1,
    )
    mine = (jnp.arange(experts, dtype=jnp.int32) == me).astype(f32)
    y_at, c_at = lax.axis_index("y"), lax.axis_index("c")
    j_at = 2 * lax.axis_index("zh") + lax.axis_index("a")
    place = jnp.arange(3, dtype=jnp.int32)
    where = jnp.where(place == 0, y_at, jnp.where(place == 1, j_at, c_at)).astype(jnp.int32)

    def settle():
        arrived = lax.all_to_all(send, GROUP, 0, 0, tiled=True)
        routed = arrived[:, :capacity, :width].reshape(rows, width)
        marked = arrived[:, :capacity, width : width + pictures].reshape(rows, pictures)
        marked = marked.astype(f32)
        own_text = arrived[:, capacity : capacity + images, :width].reshape(pictures, width)
        old_text = arrived[:, capacity + images :, :width].reshape(pictures, width)
        logits = jnp.dot(routed, router, preferred_element_type=f32)
        gates = jax.nn.sigmoid(jnp.sum(logits * mine[None, :], axis=1))
        router_row = jnp.sum(router.astype(f32) * mine[None, :], axis=1)[None, :]
        mix = lax.dot_general(
            jnp.eye(pictures, dtype=f32),
            marked * gates[:, None],
            (((1,), (1,)), ((), ())),
            precision=highest,
        )
        text_units, text_scales = unit_rows(
            jnp.concatenate([own_text, old_text], axis=0).astype(f32)
        )
        at_row = jnp.arange(pictures, dtype=jnp.int32)[:, None]
        at_col = jnp.arange(2 * pictures, dtype=jnp.int32)[None, :]
        paired = (at_row // images == (at_col % pictures) // images).astype(f32)
        label = (at_row == at_col).astype(f32)
        return routed, marked, gates, router_row, mix, text_units, text_scales, where, paired, label

    arrays, parts, settled = gathered_weights(w_in, w_out, settle)
    routed, marked, gates, router_row, mix, text_units, text_scales, where, paired, label = settled

    weight_scratch = [pltpu.VMEM((width, hidden_width), bf16)] * 2
    hidden, out, part = pl.pallas_call(
        functools.partial(forward_kernel, parts, len(arrays)),
        out_shape=(
            jax.ShapeDtypeStruct((rows, hidden_width), f32),
            jax.ShapeDtypeStruct((rows, width), bf16),
            jax.ShapeDtypeStruct((experts, pictures, width), bf16),
        ),
        in_specs=[SMEM, VMEM, VMEM] + [ANY] * len(arrays),
        out_specs=(VMEM, VMEM, VMEM),
        scratch_shapes=weight_scratch
        + [pltpu.VMEM((rows, hidden_width), bf16), pltpu.SemaphoreType.DMA((2,))],
        name="forward",
    )(where, routed, mix, *arrays)

    shared = lax.all_to_all(part, GROUP, 0, 0, tiled=True)
    out_float = out.astype(f32)
    pooled = jnp.sum(shared.astype(f32), axis=0) / patch

    units, pooled_scale = unit_rows(pooled)
    scores = temper * lax.dot_general(
        units, text_units, (((1,), (1,)), ((), ())), precision=highest
    ) + offset
    pulls = paired * (loss_scale * (jax.nn.sigmoid(scores) - label))
    grad_image = temper * jnp.dot(pulls, text_units, precision=highest)
    grad_pooled = (
        grad_image - units * jnp.sum(units * grad_image, axis=1, keepdims=True)
    ) * pooled_scale
    grad_branch = grad_pooled / patch

    spread = jnp.dot(marked, grad_branch, precision=highest)
    grad_out = (gates[:, None] * spread).astype(bf16)
    grad_gate = jnp.sum(spread * out_float, axis=1)
    grad_logit = grad_gate * gates * (1.0 - gates)
    column = jnp.dot(grad_logit[None, :], routed.astype(f32), precision=highest)
    columns = share(column.reshape(8, width // 8), OWNERS, 64)
    column = jnp.sum(columns, axis=0).reshape(1, width)
    high = column.astype(bf16)
    rest = column - high.astype(f32)
    middle = rest.astype(bf16)
    low = (rest - middle.astype(f32)).astype(bf16)

    back = pl.pallas_call(
        functools.partial(backward_kernel, parts, len(arrays)),
        out_shape=jax.ShapeDtypeStruct((experts, capacity + 8, width), bf16),
        in_specs=[SMEM, VMEM, VMEM, VMEM, VMEM] + [ANY] * len(arrays),
        out_specs=VMEM,
        scratch_shapes=weight_scratch
        + [pltpu.VMEM((rows, hidden_width), bf16), pltpu.SemaphoreType.DMA((2,))],
        name="backward",
    )(where, grad_out, hidden, grad_logit[:, None], router_row, *arrays)
    tail = jnp.concatenate([high, middle, low, jnp.zeros((5, width), bf16)], axis=0)
    tail = jnp.broadcast_to(tail[None], (experts,) + tail.shape)
    back = lax.dynamic_update_slice(back, tail, (0, capacity, 0))
    back = lax.all_to_all(back, GROUP, 0, 0, tiled=True)
    d_tokens = lax.dot_general(
        picks,
        back[:, :capacity].reshape(slot_total, width),
        (((0,), (0,)), ((), ())),
        preferred_element_type=f32,
    ).astype(bf16)
    router_grad = jnp.sum(back[:, capacity : capacity + 3].astype(f32), axis=1).T

    text_pulls = temper * lax.dot_general(
        pulls, units, (((0,), (0,)), ((), ())), precision=highest
    )
    own_pull = lax.dynamic_slice_in_dim(text_pulls, me * images, images)
    old_pull = lax.dynamic_slice_in_dim(text_pulls, pictures + me * images, images)
    own_unit = lax.dynamic_slice_in_dim(text_units, me * images, images)
    own_scale = lax.dynamic_slice_in_dim(text_scales, me * images, images)
    grad_text = own_pull + lax.ppermute(
        old_pull, DP, [((i + 1) % 64, i) for i in range(64)]
    )
    d_texts = (
        grad_text - own_unit * jnp.sum(own_unit * grad_text, axis=1, keepdims=True)
    ) * own_scale
    return d_tokens, d_texts, router_grad


def solution(mesh):
    fine = Mesh(mesh.devices.reshape(2, 2, 8, 2, 4, 2), AXES)
    block = P(AXES, None)
    flat = P(AXES)
    in_specs = (
        block,
        flat,
        flat,
        P(),
        P(("x", "zh"), DP, None),
        P(("x", "zh"), None, DP),
        block,
    )
    out_specs = (block, block, P())
    return jax.shard_map(layer, mesh=fine, in_specs=in_specs, out_specs=out_specs, check_vma=False)
```

profile of v0, /device:TPU:1, one launch (start us, length us, event | category | flops | bytes accessed | tf_op | source)
XLA Modules:
  0.0 174.0 jit_solution(7918208640491224788)
XLA Ops:
  0.6 4.6 %collective-permute-start.7 = (bf16[4,1024]{1,0:T(4,128)(2,1)}, bf16[4,1024]{1,0:T(4,128)(2,1)S(1)}, u32[]{:S(2)}, u32[]{:S(2)}) collective-permute-start(bf16[4,1024]{1,0:T(4,128)(2,1)} %param.13), channel_id=1, source_target_pairs={{0,8},{8,16},{16,24},{24,32},{32,40},{40,48},{48,56},{56,64},{64,7... | collective-permute-start | bytes 24584 | tf_op jit(solution)/shard_map/ppermute | solution.py:176
  6.1 6.1 %collective-permute-start = (bf16[32,2048]{1,0:T(8,128)(2,1)S(1)}, bf16[32,2048]{1,0:T(8,128)(2,1)S(1)}, u32[]{:S(2)}, u32[]{:S(2)}) collective-permute-start(bf16[32,2048]{1,0:T(8,128)(2,1)S(1)} %get-tuple-element.36), channel_id=1, source_target_pairs={{0,8},{8,0},{1,9},{9,1},{2,10},{10,2},{3,11},{11,3},{4,12},{12,4},... | collective-permute-start | bytes 393224 | tf_op jit(solution)/shard_map/ppermute | solution.py:50
  14.6 6.5 %collective-permute-start.1 = (bf16[2,32,2048]{2,1,0:T(8,128)(2,1)S(1)}, bf16[2,32,2048]{2,1,0:T(8,128)(2,1)S(1)}, u32[]{:S(2)}, u32[]{:S(2)}) collective-permute-start(bf16[2,32,2048]{2,1,0:T(8,128)(2,1)S(1)} %pad_maximum_fusion.1), channel_id=1, source_target_pairs={{0,0},{128,256},{256,1},{384,257},{1,128},{129,384},{257,129},{385... | collective-permute-start | bytes 786440 | tf_op jit(solution)/shard_map/ppermute | solution.py:135
  24.0 5.3 %all-to-all-start = ((bf16[8,48,1152]{2,1,0:T(8,128)(2,1)}), bf16[8,48,1152]{2,1,0:T(8,128)(2,1)S(1)}, u32[]{:S(2)}, u32[]{:S(2)}) async-start(bf16[8,48,1152]{2,1,0:T(8,128)(2,1)} %pad_maximum_fusion), calls=%async_computation | async-start | bytes 1769472 | tf_op jit(solution)/shard_map/all_to_all | solution.py:198
  29.3 3.2 %collective-permute-done.1 = bf16[2,32,2048]{2,1,0:T(8,128)(2,1)S(1)} collective-permute-done((bf16[2,32,2048]{2,1,0:T(8,128)(2,1)S(1)}, bf16[2,32,2048]{2,1,0:T(8,128)(2,1)S(1)}, u32[]{:S(2)}, u32[]{:S(2)}) %collective-permute-start.1) | collective-permute-done | bytes 262176 | tf_op jit(solution)/shard_map/ppermute | solution.py:135
  32.5 4.2 %collective-permute-start.3 = (bf16[4,32,2048]{2,1,0:T(8,128)(2,1)S(1)}, bf16[4,32,2048]{2,1,0:T(8,128)(2,1)S(1)}, u32[]{:S(2)}, u32[]{:S(2)}) collective-permute-start(bf16[4,32,2048]{2,1,0:T(8,128)(2,1)S(1)} %constant_dynamic-update-slice_fusion.rest_0_), channel_id=1, source_target_pairs={{0,16},{16,32},{32,48},{48,64},{64,80},{80,96},{96,112},{112,0},{8... | collective-permute-start | bytes 1572872 | tf_op jit(solution)/shard_map/ppermute | solution.py:141
  38.7 4.1 %collective-permute-done.3.rest_2_ = bf16[4,32,2048]{2,1,0:T(8,128)(2,1)S(1)} collective-permute-done((bf16[4,32,2048]{2,1,0:T(8,128)(2,1)S(1)}, bf16[4,32,2048]{2,1,0:T(8,128)(2,1)S(1)}, u32[]{:S(2)}, u32[]{:S(2)}) %collective-permute-start.3) | collective-permute-done | bytes 524320 | tf_op jit(solution)/shard_map/ppermute | solution.py:141
  42.8 5.2 %collective-permute-start.4 = (bf16[4,32,2048]{2,1,0:T(8,128)(2,1)S(1)}, bf16[4,32,2048]{2,1,0:T(8,128)(2,1)}, u32[]{:S(2)}, u32[]{:S(2)}) collective-permute-start(bf16[4,32,2048]{2,1,0:T(8,128)(2,1)S(1)} %collective-permute-done.3.rest_2_), channel_id=1, source_target_pairs={{0,16},{16,32},{32,48},{48,64},{64,80},{80,96},{96,112},{112,0},{8... | collective-permute-start | bytes 1572872 | tf_op jit(solution)/shard_map/ppermute | solution.py:141
  51.3 3.3 %collective-permute-start.9 = (bf16[4,32,2048]{2,1,0:T(8,128)(2,1)S(1)}, bf16[4,32,2048]{2,1,0:T(8,128)(2,1)}, u32[]{:S(2)}, u32[]{:S(2)}) collective-permute-start(bf16[4,32,2048]{2,1,0:T(8,128)(2,1)S(1)} %collective-permute-done.3.rest_2_), channel_id=1, source_target_pairs={{0,8},{8,0},{1,9},{9,1},{2,10},{10,2},{3,11},{11,3},{4,12},{12,4},... | collective-permute-start | bytes 1572872 | tf_op jit(solution)/shard_map/ppermute | solution.py:50
  54.6 4.7 %collective-permute-start.5 = (bf16[4,32,2048]{2,1,0:T(8,128)(2,1)}, bf16[4,32,2048]{2,1,0:T(8,128)(2,1)}, u32[]{:S(2)}, u32[]{:S(2)}) collective-permute-start(bf16[4,32,2048]{2,1,0:T(8,128)(2,1)} %collective-permute-done.4.rest_6_), channel_id=1, source_target_pairs={{0,16},{16,32},{32,48},{48,64},{64,80},{80,96},{96,112},{112,0},{8... | collective-permute-start | bytes 1572872 | tf_op jit(solution)/shard_map/ppermute | solution.py:141
  59.3 2.3 %collective-permute-start.12 = (bf16[4,32,2048]{2,1,0:T(8,128)(2,1)}, bf16[4,32,2048]{2,1,0:T(8,128)(2,1)}, u32[]{:S(2)}, u32[]{:S(2)}) collective-permute-start(bf16[4,32,2048]{2,1,0:T(8,128)(2,1)} %collective-permute-done.4.rest_6_), channel_id=1, source_target_pairs={{0,8},{8,0},{1,9},{9,1},{2,10},{10,2},{3,11},{11,3},{4,12},{12,4},... | collective-permute-start | bytes 1572872 | tf_op jit(solution)/shard_map/ppermute | solution.py:50
  61.6 4.9 %collective-permute-start.13 = (bf16[4,32,2048]{2,1,0:T(8,128)(2,1)}, bf16[4,32,2048]{2,1,0:T(8,128)(2,1)}, u32[]{:S(2)}, u32[]{:S(2)}) collective-permute-start(bf16[4,32,2048]{2,1,0:T(8,128)(2,1)} %collective-permute-done.10.rest_4_), channel_id=1, source_target_pairs={{0,16},{16,32},{32,48},{48,64},{64,80},{80,96},{96,112},{112,0},{8... | collective-permute-start | bytes 1572872 | tf_op jit(solution)/shard_map/ppermute | solution.py:141
  69.2 3.7 %collective-permute-start.6 = (bf16[4,32,2048]{2,1,0:T(8,128)(2,1)}, bf16[4,32,2048]{2,1,0:T(8,128)(2,1)S(1)}, u32[]{:S(2)}, u32[]{:S(2)}) collective-permute-start(bf16[4,32,2048]{2,1,0:T(8,128)(2,1)} %collective-permute-done.5.rest_10_), channel_id=1, source_target_pairs={{0,16},{16,32},{32,48},{48,64},{64,80},{80,96},{96,112},{112,0},{8... | collective-permute-start | bytes 1572872 | tf_op jit(solution)/shard_map/ppermute | solution.py:141
  72.9 5.0 %collective-permute-start.16 = (bf16[4,32,2048]{2,1,0:T(8,128)(2,1)}, bf16[4,32,2048]{2,1,0:T(8,128)(2,1)S(1)}, u32[]{:S(2)}, u32[]{:S(2)}) collective-permute-start(bf16[4,32,2048]{2,1,0:T(8,128)(2,1)} %collective-permute-done.13.rest_8_), channel_id=1, source_target_pairs={{0,16},{16,32},{32,48},{48,64},{64,80},{80,96},{96,112},{112,0},{8... | collective-permute-start | bytes 1572872 | tf_op jit(solution)/shard_map/ppermute | solution.py:141
  79.6 5.1 %collective-permute-start.15 = (bf16[4,32,2048]{2,1,0:T(8,128)(2,1)}, bf16[4,32,2048]{2,1,0:T(8,128)(2,1)S(1)}, u32[]{:S(2)}, u32[]{:S(2)}) collective-permute-start(bf16[4,32,2048]{2,1,0:T(8,128)(2,1)} %collective-permute-done.5.rest_10_), channel_id=1, source_target_pairs={{0,8},{8,0},{1,9},{9,1},{2,10},{10,2},{3,11},{11,3},{4,12},{12,4},... | collective-permute-start | bytes 1572872 | tf_op jit(solution)/shard_map/ppermute | solution.py:50
  86.7 2.4 %collective-permute-start.18 = (bf16[4,32,2048]{2,1,0:T(8,128)(2,1)S(1)}, bf16[4,32,2048]{2,1,0:T(8,128)(2,1)S(1)}, u32[]{:S(2)}, u32[]{:S(2)}) collective-permute-start(bf16[4,32,2048]{2,1,0:T(8,128)(2,1)S(1)} %collective-permute-done.6.rest_14_), channel_id=1, source_target_pairs={{0,8},{8,0},{1,9},{9,1},{2,10},{10,2},{3,11},{11,3},{4,12},{12,4},... | collective-permute-start | bytes 1572872 | tf_op jit(solution)/shard_map/ppermute | solution.py:50
  93.1 10.6 %forward.1 = (f32[320,2048]{1,0:T(8,128)}, bf16[320,1024]{1,0:T(8,128)(2,1)}, bf16[8,32,1024]{2,1,0:T(8,128)(2,1)}) custom-call(s32[3]{0:T(128)} %compare_select_fusion.1.where, bf16[320,1024]{1,0:T(8,128)(2,1)} %bitcast.38, f32[32,320]{1,0:T(8,128)} %fusion.15.mix_ref, bf16[4,32,2048]{2,1,0:T(8,128)(2,1)} %copy-done.2, bf16[4,32,2048]{2,1,0:T(8,128)(2,1)} %copy-done.4, ...), custom_call_target="tpu_custom_call" | custom-call | tf_op jit(solution)/shard_map/forward/pallas_call | solution.py:226
  103.7 18.6 %all_to_all.20 = bf16[8,32,1024]{2,1,0:T(8,128)(2,1)S(1)} all-to-all(bf16[8,32,1024]{2,1,0:T(8,128)(2,1)} %get-tuple-element.24), channel_id=1, replica_groups=mesh['a'=2,'b'=2,'y'=8,'c'=2,'x'=4,'zh'=2] {'x','b'}, dimensions={0} | all-to-all | bytes 1048576 | tf_op jit(solution)/shard_map/all_to_all | solution.py:240
  126.8 13.9 %all-to-all-start.2 = ((f32[64,8,128]{2,1,0:T(8,128)}), f32[64,8,128]{2,1,0:T(8,128)S(1)}, u32[]{:S(2)}, u32[]{:S(2)}) async-start(f32[64,8,128]{2,1,0:T(8,128)} %broadcast_in_dim.35), calls=%async_computation.2 | async-start | bytes 524288 | tf_op jit(solution)/shard_map/all_to_all | solution.py:153
  141.5 9.2 %backward.1 = bf16[8,48,1024]{2,1,0:T(8,128)(2,1)} custom-call(s32[3]{0:T(128)} %compare_select_fusion.1.where, bf16[320,1024]{1,0:T(8,128)(2,1)} %get-tuple-element.32.dy_ref, f32[320,2048]{1,0:T(8,128)} %get-tuple-element.27.hid_ref, f32[320,1]{1,0:T(8,128)} %broadcast_in_dim.67.grad_logit, f32[1,1024]{1,0:T(1,128)} %bitcast.49, ...), custom_call_target="tpu_custom_call" | custom-call | tf_op jit(solution)/shard_map/backward/pallas_call | solution.py:267
  150.7 4.2 %all-to-all-done.2 = f32[64,8,128]{2,1,0:T(8,128)S(1)} async-done(((f32[64,8,128]{2,1,0:T(8,128)}), f32[64,8,128]{2,1,0:T(8,128)S(1)}, u32[]{:S(2)}, u32[]{:S(2)}) %all-to-all-start.2) | async-done | bytes 262176 | tf_op jit(solution)/shard_map/all_to_all | solution.py:153
  155.7 3.5 %all-to-all-start.3 = ((bf16[8,48,1024]{2,1,0:T(8,128)(2,1)}), bf16[8,48,1024]{2,1,0:T(8,128)(2,1)S(1)}, u32[]{:S(2)}, u32[]{:S(2)}) async-start(bf16[8,48,1024]{2,1,0:T(8,128)(2,1)} %broadcast_dynamic-update-slice_fusion), calls=%async_computation.3 | async-start | bytes 1572864 | tf_op jit(solution)/shard_map/all_to_all | solution.py:279
  162.1 3.0 %collective-permute-done.19 = f32[4,1024]{1,0:T(4,128)S(1)} collective-permute-done((f32[4,1024]{1,0:T(4,128)S(1)}, f32[4,1024]{1,0:T(4,128)S(1)}, u32[]{:S(2)}, u32[]{:S(2)}) %collective-permute-start.19) | collective-permute-done | bytes 16416 | tf_op jit(solution)/shard_map/ppermute | solution.py:295
  165.9 6.0 %all-to-all-done.3 = bf16[8,48,1024]{2,1,0:T(8,128)(2,1)S(1)} async-done(((bf16[8,48,1024]{2,1,0:T(8,128)(2,1)}), bf16[8,48,1024]{2,1,0:T(8,128)(2,1)S(1)}, u32[]{:S(2)}, u32[]{:S(2)}) %all-to-all-start.3) | async-done | bytes 786464 | tf_op jit(solution)/shard_map/all_to_all | solution.py:279
  (106 shorter events, 33.1 us)
Async XLA Ops:
  0.6 13.8 %collective-permute-start.7 = (bf16[4,1024]{1,0:T(4,128)(2,1)}, bf16[4,1024]{1,0:T(4,128)(2,1)S(1)}, u32[]{:S(2)}, u32[]{:S(2)}) collective-permute-start(bf16[4,1024]{1,0:T(4,128)(2,1)} %param.13), channel_id=1, source_target_pairs={{0,8},{8,16},{16,24},{24,32},{32,40},{40,48},{48,56},{56,64},{64,7... | collective-permute-start | bytes 24584 | tf_op jit(solution)/shard_map/ppermute | solution.py:176
  6.1 8.4 %collective-permute-start = (bf16[32,2048]{1,0:T(8,128)(2,1)S(1)}, bf16[32,2048]{1,0:T(8,128)(2,1)S(1)}, u32[]{:S(2)}, u32[]{:S(2)}) collective-permute-start(bf16[32,2048]{1,0:T(8,128)(2,1)S(1)} %get-tuple-element.36), channel_id=1, source_target_pairs={{0,8},{8,0},{1,9},{9,1},{2,10},{10,2},{3,11},{11,3},{4,12},{12,4},... | collective-permute-start | bytes 393224 | tf_op jit(solution)/shard_map/ppermute | solution.py:50
  14.6 17.9 %collective-permute-start.1 = (bf16[2,32,2048]{2,1,0:T(8,128)(2,1)S(1)}, bf16[2,32,2048]{2,1,0:T(8,128)(2,1)S(1)}, u32[]{:S(2)}, u32[]{:S(2)}) collective-permute-start(bf16[2,32,2048]{2,1,0:T(8,128)(2,1)S(1)} %pad_maximum_fusion.1), channel_id=1, source_target_pairs={{0,0},{128,256},{256,1},{384,257},{1,128},{129,384},{257,129},{385... | collective-permute-start | bytes 786440 | tf_op jit(solution)/shard_map/ppermute | solution.py:135
  21.0 11.4 %collective-permute-start.2 = (bf16[2,32,2048]{2,1,0:T(8,128)(2,1)S(1)}, bf16[2,32,2048]{2,1,0:T(8,128)(2,1)S(1)}, u32[]{:S(2)}, u32[]{:S(2)}) collective-permute-start(bf16[2,32,2048]{2,1,0:T(8,128)(2,1)S(1)} %pad_maximum_fusion.1), channel_id=1, source_target_pairs={{0,256},{128,1},{256,257},{384,0},{1,384},{129,129},{257,385},{385... | collective-permute-start | bytes 786440 | tf_op jit(solution)/shard_map/ppermute | solution.py:135
  24.0 44.4 %all-to-all-start = ((bf16[8,48,1152]{2,1,0:T(8,128)(2,1)}), bf16[8,48,1152]{2,1,0:T(8,128)(2,1)S(1)}, u32[]{:S(2)}, u32[]{:S(2)}) async-start(bf16[8,48,1152]{2,1,0:T(8,128)(2,1)} %pad_maximum_fusion), calls=%async_computation | async-start | bytes 1769472 | tf_op jit(solution)/shard_map/all_to_all | solution.py:198
  32.5 36.4 %copy-start.2 = (bf16[4,32,2048]{2,1,0:T(8,128)(2,1)}, bf16[4,32,2048]{2,1,0:T(8,128)(2,1)S(1)}, u32[]{:S(2)}) copy-start(bf16[4,32,2048]{2,1,0:T(8,128)(2,1)S(1)} %constant_dynamic-update-slice_fusion.rest_0_) | copy-start | bytes 1572868
  32.5 10.3 %collective-permute-start.3 = (bf16[4,32,2048]{2,1,0:T(8,128)(2,1)S(1)}, bf16[4,32,2048]{2,1,0:T(8,128)(2,1)S(1)}, u32[]{:S(2)}, u32[]{:S(2)}) collective-permute-start(bf16[4,32,2048]{2,1,0:T(8,128)(2,1)S(1)} %constant_dynamic-update-slice_fusion.rest_0_), channel_id=1, source_target_pairs={{0,16},{16,32},{32,48},{48,64},{64,80},{80,96},{96,112},{112,0},{8... | collective-permute-start | bytes 1572872 | tf_op jit(solution)/shard_map/ppermute | solution.py:141
  36.7 11.4 %collective-permute-start.8 = (bf16[4,32,2048]{2,1,0:T(8,128)(2,1)S(1)}, bf16[4,32,2048]{2,1,0:T(8,128)(2,1)S(1)}, u32[]{:S(2)}, u32[]{:S(2)}) collective-permute-start(bf16[4,32,2048]{2,1,0:T(8,128)(2,1)S(1)} %constant_dynamic-update-slice_fusion.rest_0_), channel_id=1, source_target_pairs={{0,8},{8,0},{1,9},{9,1},{2,10},{10,2},{3,11},{11,3},{4,12},{12,4},... | collective-permute-start | bytes 1572872 | tf_op jit(solution)/shard_map/ppermute | solution.py:50
  42.8 11.8 %collective-permute-start.4 = (bf16[4,32,2048]{2,1,0:T(8,128)(2,1)S(1)}, bf16[4,32,2048]{2,1,0:T(8,128)(2,1)}, u32[]{:S(2)}, u32[]{:S(2)}) collective-permute-start(bf16[4,32,2048]{2,1,0:T(8,128)(2,1)S(1)} %collective-permute-done.3.rest_2_), channel_id=1, source_target_pairs={{0,16},{16,32},{32,48},{48,64},{64,80},{80,96},{96,112},{112,0},{8... | collective-permute-start | bytes 1572872 | tf_op jit(solution)/shard_map/ppermute | solution.py:141
  48.1 13.5 %collective-permute-start.10 = (bf16[4,32,2048]{2,1,0:T(8,128)(2,1)S(1)}, bf16[4,32,2048]{2,1,0:T(8,128)(2,1)}, u32[]{:S(2)}, u32[]{:S(2)}) collective-permute-start(bf16[4,32,2048]{2,1,0:T(8,128)(2,1)S(1)} %collective-permute-done.8.rest_1_), channel_id=1, source_target_pairs={{0,16},{16,32},{32,48},{48,64},{64,80},{80,96},{96,112},{112,0},{8... | collective-permute-start | bytes 1572872 | tf_op jit(solution)/shard_map/ppermute | solution.py:141
  51.3 33.5 %collective-permute-start.9 = (bf16[4,32,2048]{2,1,0:T(8,128)(2,1)S(1)}, bf16[4,32,2048]{2,1,0:T(8,128)(2,1)}, u32[]{:S(2)}, u32[]{:S(2)}) collective-permute-start(bf16[4,32,2048]{2,1,0:T(8,128)(2,1)S(1)} %collective-permute-done.3.rest_2_), channel_id=1, source_target_pairs={{0,8},{8,0},{1,9},{9,1},{2,10},{10,2},{3,11},{11,3},{4,12},{12,4},... | collective-permute-start | bytes 1572872 | tf_op jit(solution)/shard_map/ppermute | solution.py:50
  54.6 14.6 %collective-permute-start.5 = (bf16[4,32,2048]{2,1,0:T(8,128)(2,1)}, bf16[4,32,2048]{2,1,0:T(8,128)(2,1)}, u32[]{:S(2)}, u32[]{:S(2)}) collective-permute-start(bf16[4,32,2048]{2,1,0:T(8,128)(2,1)} %collective-permute-done.4.rest_6_), channel_id=1, source_target_pairs={{0,16},{16,32},{32,48},{48,64},{64,80},{80,96},{96,112},{112,0},{8... | collective-permute-start | bytes 1572872 | tf_op jit(solution)/shard_map/ppermute | solution.py:141
  59.3 27.4 %collective-permute-start.12 = (bf16[4,32,2048]{2,1,0:T(8,128)(2,1)}, bf16[4,32,2048]{2,1,0:T(8,128)(2,1)}, u32[]{:S(2)}, u32[]{:S(2)}) collective-permute-start(bf16[4,32,2048]{2,1,0:T(8,128)(2,1)} %collective-permute-done.4.rest_6_), channel_id=1, source_target_pairs={{0,8},{8,0},{1,9},{9,1},{2,10},{10,2},{3,11},{11,3},{4,12},{12,4},... | collective-permute-start | bytes 1572872 | tf_op jit(solution)/shard_map/ppermute | solution.py:50
  61.6 11.3 %collective-permute-start.13 = (bf16[4,32,2048]{2,1,0:T(8,128)(2,1)}, bf16[4,32,2048]{2,1,0:T(8,128)(2,1)}, u32[]{:S(2)}, u32[]{:S(2)}) collective-permute-start(bf16[4,32,2048]{2,1,0:T(8,128)(2,1)} %collective-permute-done.10.rest_4_), channel_id=1, source_target_pairs={{0,16},{16,32},{32,48},{48,64},{64,80},{80,96},{96,112},{112,0},{8... | collective-permute-start | bytes 1572872 | tf_op jit(solution)/shard_map/ppermute | solution.py:141
  66.5 24.6 %collective-permute-start.11 = (bf16[4,32,2048]{2,1,0:T(8,128)(2,1)}, bf16[4,32,2048]{2,1,0:T(8,128)(2,1)}, u32[]{:S(2)}, u32[]{:S(2)}) collective-permute-start(bf16[4,32,2048]{2,1,0:T(8,128)(2,1)} %collective-permute-done.10.rest_4_), channel_id=1, source_target_pairs={{0,8},{8,0},{1,9},{9,1},{2,10},{10,2},{3,11},{11,3},{4,12},{12,4},... | collective-permute-start | bytes 1572872 | tf_op jit(solution)/shard_map/ppermute | solution.py:50
  69.2 10.4 %collective-permute-start.6 = (bf16[4,32,2048]{2,1,0:T(8,128)(2,1)}, bf16[4,32,2048]{2,1,0:T(8,128)(2,1)S(1)}, u32[]{:S(2)}, u32[]{:S(2)}) collective-permute-start(bf16[4,32,2048]{2,1,0:T(8,128)(2,1)} %collective-permute-done.5.rest_10_), channel_id=1, source_target_pairs={{0,16},{16,32},{32,48},{48,64},{64,80},{80,96},{96,112},{112,0},{8... | collective-permute-start | bytes 1572872 | tf_op jit(solution)/shard_map/ppermute | solution.py:141
  72.9 16.2 %collective-permute-start.16 = (bf16[4,32,2048]{2,1,0:T(8,128)(2,1)}, bf16[4,32,2048]{2,1,0:T(8,128)(2,1)S(1)}, u32[]{:S(2)}, u32[]{:S(2)}) collective-permute-start(bf16[4,32,2048]{2,1,0:T(8,128)(2,1)} %collective-permute-done.13.rest_8_), channel_id=1, source_target_pairs={{0,16},{16,32},{32,48},{48,64},{64,80},{80,96},{96,112},{112,0},{8... | collective-permute-start | bytes 1572872 | tf_op jit(solution)/shard_map/ppermute | solution.py:141
  79.6 11.5 %collective-permute-start.15 = (bf16[4,32,2048]{2,1,0:T(8,128)(2,1)}, bf16[4,32,2048]{2,1,0:T(8,128)(2,1)S(1)}, u32[]{:S(2)}, u32[]{:S(2)}) collective-permute-start(bf16[4,32,2048]{2,1,0:T(8,128)(2,1)} %collective-permute-done.5.rest_10_), channel_id=1, source_target_pairs={{0,8},{8,0},{1,9},{9,1},{2,10},{10,2},{3,11},{11,3},{4,12},{12,4},... | collective-permute-start | bytes 1572872 | tf_op jit(solution)/shard_map/ppermute | solution.py:50
  84.7 6.3 %collective-permute-start.14 = (bf16[4,32,2048]{2,1,0:T(8,128)(2,1)}, bf16[4,32,2048]{2,1,0:T(8,128)(2,1)S(1)}, u32[]{:S(2)}, u32[]{:S(2)}) collective-permute-start(bf16[4,32,2048]{2,1,0:T(8,128)(2,1)} %collective-permute-done.13.rest_8_), channel_id=1, source_target_pairs={{0,8},{8,0},{1,9},{9,1},{2,10},{10,2},{3,11},{11,3},{4,12},{12,4},... | collective-permute-start | bytes 1572872 | tf_op jit(solution)/shard_map/ppermute | solution.py:50
  86.7 4.4 %collective-permute-start.18 = (bf16[4,32,2048]{2,1,0:T(8,128)(2,1)S(1)}, bf16[4,32,2048]{2,1,0:T(8,128)(2,1)S(1)}, u32[]{:S(2)}, u32[]{:S(2)}) collective-permute-start(bf16[4,32,2048]{2,1,0:T(8,128)(2,1)S(1)} %collective-permute-done.6.rest_14_), channel_id=1, source_target_pairs={{0,8},{8,0},{1,9},{9,1},{2,10},{10,2},{3,11},{11,3},{4,12},{12,4},... | collective-permute-start | bytes 1572872 | tf_op jit(solution)/shard_map/ppermute | solution.py:50
  89.1 3.9 %collective-permute-start.17 = (bf16[4,32,2048]{2,1,0:T(8,128)(2,1)S(1)}, bf16[4,32,2048]{2,1,0:T(8,128)(2,1)}, u32[]{:S(2)}, u32[]{:S(2)}) collective-permute-start(bf16[4,32,2048]{2,1,0:T(8,128)(2,1)S(1)} %collective-permute-done.16.rest_12_), channel_id=1, source_target_pairs={{0,8},{8,0},{1,9},{9,1},{2,10},{10,2},{3,11},{11,3},{4,12},{12,4},... | collective-permute-start | bytes 1572872 | tf_op jit(solution)/shard_map/ppermute | solution.py:50
  126.8 28.1 %all-to-all-start.2 = ((f32[64,8,128]{2,1,0:T(8,128)}), f32[64,8,128]{2,1,0:T(8,128)S(1)}, u32[]{:S(2)}, u32[]{:S(2)}) async-start(f32[64,8,128]{2,1,0:T(8,128)} %broadcast_in_dim.35), calls=%async_computation.2 | async-start | bytes 524288 | tf_op jit(solution)/shard_map/all_to_all | solution.py:153
  155.7 16.2 %all-to-all-start.3 = ((bf16[8,48,1024]{2,1,0:T(8,128)(2,1)}), bf16[8,48,1024]{2,1,0:T(8,128)(2,1)S(1)}, u32[]{:S(2)}, u32[]{:S(2)}) async-start(bf16[8,48,1024]{2,1,0:T(8,128)(2,1)} %broadcast_dynamic-update-slice_fusion), calls=%async_computation.3 | async-start | bytes 1572864 | tf_op jit(solution)/shard_map/all_to_all | solution.py:279
  159.7 5.4 %collective-permute-start.19 = (f32[4,1024]{1,0:T(4,128)S(1)}, f32[4,1024]{1,0:T(4,128)S(1)}, u32[]{:S(2)}, u32[]{:S(2)}) collective-permute-start(f32[4,1024]{1,0:T(4,128)S(1)} %constant_dynamic-slice_fusion.1), channel_id=1, source_target_pairs={{8,0},{16,8},{24,16},{32,24},{40,32},{48,40},{56,48},{64,56},{72,6... | collective-permute-start | bytes 49160 | tf_op jit(solution)/shard_map/ppermute | solution.py:295
  (12 other events, 136.1 us)
where the time goes:
time: 175 us; the launch traced here: 174 us
  starting transfers between devices  94.4 us (54%)
  waiting for transfers between devices  21.7 us (12%)
  Pallas kernels  19.7 us (11%)
  blocking collectives  18.6 us (11%)
  other arithmetic  7.18 us (4%)
  matrix products  6.76 us (4%)
  local copies, waits for them, and re-layouts  4.28 us (2%)
    ppermute x7, starting transfers between devices, gathered_weights(): moved = lax.ppermute(chunks[n], ('y', 'c'), ring_route())  29.5 us
    ppermute x9, starting transfers between devices, swap_cores(): return lax.ppermute(block, 'c', [(0, 1), (1, 0)])  26.9 us
    all_to_all x1, blocking collectives, layer(): shared = lax.all_to_all(part, GROUP, 0, 0, tiled=True)  18.6 us
    all_to_all x1, starting transfers between devices, share(): lax.all_to_all(jnp.broadcast_to(block[None], (count,) + block.shape), axe...  13.9 us
    pallas_call x1, Pallas kernels, layer(): pl.pallas_call(functools.partial(forward_kernel, parts, len(arrays)), out...  10.6 us
    pallas_call x1, Pallas kernels, layer(): pl.pallas_call(functools.partial(backward_kernel, parts, len(arrays)), ou...  9.15 us
    ppermute x2, starting transfers between devices, gathered_weights(): lax.ppermute(pair, DEEP, depth_round(n))  8.41 us
    all_to_all x1, waiting for transfers between devices, layer(): back = lax.all_to_all(back, GROUP, 0, 0, tiled=True)  6.01 us
  transfers between devices with their start and end apart: 23, of which 7 were waited for; matrix products, arithmetic and copies ran while one was open for 5% of the time, Pallas kernels for 5%

commit v1 on v0

--- a/solution.py
+++ b/solution.py
@@ -75,28 +75,33 @@
 
 
 def forward_kernel(parts, count, where, x_ref, mix_ref, *rest):
-    refs, (hid_ref, out_ref, part_ref, win, wout, act, sems) = rest[:count], rest[count:]
+    refs = rest[:count]
+    hid_out, out_ref, part_ref, win, wout, act, hid, sems, hid_sems = rest[count:]
     start_copies(where, parts, refs, win, sems.at[0], 0)
     start_copies(where, parts, refs, wout, sems.at[1], 1)
     wait_all(win, sems.at[0])
+    leaving = []
     for n in range(4):
         at = slice(n * 512, n * 512 + 512)
         hidden = jnp.dot(x_ref[...], win[:, at], preferred_element_type=jnp.float32)
-        hid_ref[:, at] = hidden
+        hid[:, at] = hidden
+        copy = pltpu.make_async_copy(hid.at[:, at], hid_out.at[:, at], hid_sems.at[n])
+        copy.start()
+        leaving.append(copy)
         act[:, at] = jax.nn.gelu(hidden, approximate=True).astype(jnp.bfloat16)
     wait_all(wout, sems.at[1])
+    pictures = part_ref.shape[1]
     for n in range(4):
         at = slice(n * 256, n * 256 + 256)
         out = contract_last(act[...], wout[at, :]).astype(jnp.bfloat16)
         out_ref[:, at] = out
-        part = jnp.dot(
-            mix_ref[...],
-            out.astype(jnp.float32),
-            precision=highest,
-            preferred_element_type=jnp.float32,
-        ).astype(jnp.bfloat16)
+        thirds = jnp.dot(mix_ref[...], out, preferred_element_type=jnp.float32)
+        part = thirds[:pictures] + thirds[pictures : 2 * pictures] + thirds[2 * pictures :]
+        part = part.astype(jnp.bfloat16)
         for member in range(part_ref.shape[0]):
             part_ref[member, :, at] = part
+    for copy in leaving:
+        copy.wait()
 
 
 def gelu_slope(hidden):
@@ -107,15 +112,18 @@
     return 0.5 * (1.0 + bent) + 0.5 * hidden * (1.0 - bent * bent) * inner
 
 
-def backward_kernel(parts, count, where, dy_ref, hid_ref, grad_logit, router_row, *rest):
-    refs, (back_ref, win, wout, dhid, sems) = rest[:count], rest[count:]
+def backward_kernel(parts, count, where, dy_ref, hid_in, grad_logit, router_row, *rest):
+    refs, (back_ref, win, wout, dhid, hid, sems, hid_sem) = rest[:count], rest[count:]
     start_copies(where, parts, refs, wout, sems.at[1], 1)
+    entering = pltpu.make_async_copy(hid_in, hid, hid_sem)
+    entering.start()
     start_copies(where, parts, refs, win, sems.at[0], 0)
     wait_all(wout, sems.at[1])
+    entering.wait()
     for n in range(4):
         at = slice(n * 512, n * 512 + 512)
         grad = jnp.dot(dy_ref[...], wout[:, at], preferred_element_type=jnp.float32)
-        dhid[:, at] = (grad * gelu_slope(hid_ref[:, at])).astype(jnp.bfloat16)
+        dhid[:, at] = (grad * gelu_slope(hid[:, at])).astype(jnp.bfloat16)
     wait_all(win, sems.at[0])
     members, _, width = back_ref.shape
     capacity = dhid.shape[0] // members
@@ -155,6 +163,13 @@
     )
 
 
+def thirds_of(matrix):
+    high = lax.reduce_precision(matrix, 8, 7)
+    rest = matrix - high
+    middle = lax.reduce_precision(rest, 8, 7)
+    return tuple(x.astype(jnp.bfloat16) for x in (high, middle, rest - middle))
+
+
 def unit_rows(matrix):
     scales = lax.rsqrt(jnp.sum(matrix * matrix, axis=1, keepdims=True) + epsilon)
     return matrix * scales, scales
@@ -210,6 +225,7 @@
             (((1,), (1,)), ((), ())),
             precision=highest,
         )
+        mix = jnp.concatenate(thirds_of(mix), axis=0)
         text_units, text_scales = unit_rows(
             jnp.concatenate([own_text, old_text], axis=0).astype(f32)
         )
@@ -231,9 +247,14 @@
             jax.ShapeDtypeStruct((experts, pictures, width), bf16),
         ),
         in_specs=[SMEM, VMEM, VMEM] + [ANY] * len(arrays),
-        out_specs=(VMEM, VMEM, VMEM),
+        out_specs=(ANY, VMEM, VMEM),
         scratch_shapes=weight_scratch
-        + [pltpu.VMEM((rows, hidden_width), bf16), pltpu.SemaphoreType.DMA((2,))],
+        + [
+            pltpu.VMEM((rows, hidden_width), bf16),
+            pltpu.VMEM((rows, hidden_width), f32),
+            pltpu.SemaphoreType.DMA((2,)),
+            pltpu.SemaphoreType.DMA((4,)),
+        ],
         name="forward",
     )(where, routed, mix, *arrays)
 
@@ -259,18 +280,20 @@
     column = jnp.dot(grad_logit[None, :], routed.astype(f32), precision=highest)
     columns = share(column.reshape(8, width // 8), OWNERS, 64)
     column = jnp.sum(columns, axis=0).reshape(1, width)
-    high = column.astype(bf16)
-    rest = column - high.astype(f32)
-    middle = rest.astype(bf16)
-    low = (rest - middle.astype(f32)).astype(bf16)
+    high, middle, low = thirds_of(column)
 
     back = pl.pallas_call(
         functools.partial(backward_kernel, parts, len(arrays)),
         out_shape=jax.ShapeDtypeStruct((experts, capacity + 8, width), bf16),
-        in_specs=[SMEM, VMEM, VMEM, VMEM, VMEM] + [ANY] * len(arrays),
+        in_specs=[SMEM, VMEM, ANY, VMEM, VMEM] + [ANY] * len(arrays),
         out_specs=VMEM,
         scratch_shapes=weight_scratch
-        + [pltpu.VMEM((rows, hidden_width), bf16), pltpu.SemaphoreType.DMA((2,))],
+        + [
+            pltpu.VMEM((rows, hidden_width), bf16),
+            pltpu.VMEM((rows, hidden_width), f32),
+            pltpu.SemaphoreType.DMA((2,)),
+            pltpu.SemaphoreType.DMA,
+        ],
         name="backward",
     )(where, grad_out, hidden, grad_logit[:, None], router_row, *arrays)
     tail = jnp.concatenate([high, middle, low, jnp.zeros((5, width), bf16)], axis=0)

time: 175 us -> 175 us (level)
  transfers between devices with their start and end apart: 23 -> 23, of which waited for: 7 -> 7; matrix products, arithmetic and copies ran while one was open for 5% -> 5% of each run, Pallas kernels for 5% -> 6%
where the time goes in v1:
time: 175 us; the launch traced here: 174 us
  starting transfers between devices  93.8 us (54%)
  waiting for transfers between devices  20.7 us (12%)
  Pallas kernels  20.7 us (12%)
  blocking collectives  18.7 us (11%)
  other arithmetic  7.82 us (4%)
  matrix products  6.16 us (4%)
  local copies, waits for them, and re-layouts  4.29 us (2%)
    ppermute x7, starting transfers between devices, gathered_weights(): moved = lax.ppermute(chunks[n], ('y', 'c'), ring_route())  29.3 us
    ppermute x9, starting transfers between devices, swap_cores(): return lax.ppermute(block, 'c', [(0, 1), (1, 0)])  26.6 us
    all_to_all x1, blocking collectives, layer(): shared = lax.all_to_all(part, GROUP, 0, 0, tiled=True)  18.7 us
    all_to_all x1, starting transfers between devices, share(): lax.all_to_all(jnp.broadcast_to(block[None], (count,) + block.shape), axe...  13.9 us
    pallas_call x1, Pallas kernels, layer(): pl.pallas_call(functools.partial(backward_kernel, parts, len(arrays)), ou...  10.6 us
    pallas_call x1, Pallas kernels, layer(): pl.pallas_call(functools.partial(forward_kernel, parts, len(arrays)), out...  10.1 us
    ppermute x2, starting transfers between devices, gathered_weights(): lax.ppermute(pair, DEEP, depth_round(n))  8.41 us
    all_to_all x1, waiting for transfers between devices, layer(): back = lax.all_to_all(back, GROUP, 0, 0, tiled=True)  6.01 us
  transfers between devices with their start and end apart: 23, of which 7 were waited for; matrix products, arithmetic and copies ran while one was open for 5% of the time, Pallas kernels for 6%

profile of v1, /device:TPU:1, one launch (start us, length us, event | category | flops | bytes accessed | tf_op | source)
XLA Modules:
  0.0 173.5 jit_solution(9929034354767056917)
XLA Ops:
  0.6 4.6 %collective-permute-start.7 = (bf16[4,1024]{1,0:T(4,128)(2,1)}, bf16[4,1024]{1,0:T(4,128)(2,1)S(1)}, u32[]{:S(2)}, u32[]{:S(2)}) collective-permute-start(bf16[4,1024]{1,0:T(4,128)(2,1)} %param.13), channel_id=1, source_target_pairs={{0,8},{8,16},{16,24},{24,32},{32,40},{40,48},{48,56},{56,64},{64,7... | collective-permute-start | bytes 24584 | tf_op jit(solution)/shard_map/ppermute | solution.py:191
  6.1 6.1 %collective-permute-start = (bf16[32,2048]{1,0:T(8,128)(2,1)S(1)}, bf16[32,2048]{1,0:T(8,128)(2,1)S(1)}, u32[]{:S(2)}, u32[]{:S(2)}) collective-permute-start(bf16[32,2048]{1,0:T(8,128)(2,1)S(1)} %get-tuple-element.36), channel_id=1, source_target_pairs={{0,8},{8,0},{1,9},{9,1},{2,10},{10,2},{3,11},{11,3},{4,12},{12,4},... | collective-permute-start | bytes 393224 | tf_op jit(solution)/shard_map/ppermute | solution.py:50
  14.6 6.5 %collective-permute-start.1 = (bf16[2,32,2048]{2,1,0:T(8,128)(2,1)S(1)}, bf16[2,32,2048]{2,1,0:T(8,128)(2,1)S(1)}, u32[]{:S(2)}, u32[]{:S(2)}) collective-permute-start(bf16[2,32,2048]{2,1,0:T(8,128)(2,1)S(1)} %pad_maximum_fusion.1), channel_id=1, source_target_pairs={{0,0},{128,256},{256,1},{384,257},{1,128},{129,384},{257,129},{385... | collective-permute-start | bytes 786440 | tf_op jit(solution)/shard_map/ppermute | solution.py:143
  24.0 5.3 %all-to-all-start = ((bf16[8,48,1152]{2,1,0:T(8,128)(2,1)}), bf16[8,48,1152]{2,1,0:T(8,128)(2,1)S(1)}, u32[]{:S(2)}, u32[]{:S(2)}) async-start(bf16[8,48,1152]{2,1,0:T(8,128)(2,1)} %pad_maximum_fusion), calls=%async_computation | async-start | bytes 1769472 | tf_op jit(solution)/shard_map/all_to_all | solution.py:213
  29.3 3.1 %collective-permute-done.1 = bf16[2,32,2048]{2,1,0:T(8,128)(2,1)S(1)} collective-permute-done((bf16[2,32,2048]{2,1,0:T(8,128)(2,1)S(1)}, bf16[2,32,2048]{2,1,0:T(8,128)(2,1)S(1)}, u32[]{:S(2)}, u32[]{:S(2)}) %collective-permute-start.1) | collective-permute-done | bytes 262176 | tf_op jit(solution)/shard_map/ppermute | solution.py:143
  32.5 4.2 %collective-permute-start.3 = (bf16[4,32,2048]{2,1,0:T(8,128)(2,1)S(1)}, bf16[4,32,2048]{2,1,0:T(8,128)(2,1)S(1)}, u32[]{:S(2)}, u32[]{:S(2)}) collective-permute-start(bf16[4,32,2048]{2,1,0:T(8,128)(2,1)S(1)} %constant_dynamic-update-slice_fusion.rest_0_), channel_id=1, source_target_pairs={{0,16},{16,32},{32,48},{48,64},{64,80},{80,96},{96,112},{112,0},{8... | collective-permute-start | bytes 1572872 | tf_op jit(solution)/shard_map/ppermute | solution.py:149
  38.7 4.1 %collective-permute-done.3.rest_2_ = bf16[4,32,2048]{2,1,0:T(8,128)(2,1)S(1)} collective-permute-done((bf16[4,32,2048]{2,1,0:T(8,128)(2,1)S(1)}, bf16[4,32,2048]{2,1,0:T(8,128)(2,1)S(1)}, u32[]{:S(2)}, u32[]{:S(2)}) %collective-permute-start.3) | collective-permute-done | bytes 524320 | tf_op jit(solution)/shard_map/ppermute | solution.py:149
  42.8 5.3 %collective-permute-start.4 = (bf16[4,32,2048]{2,1,0:T(8,128)(2,1)S(1)}, bf16[4,32,2048]{2,1,0:T(8,128)(2,1)}, u32[]{:S(2)}, u32[]{:S(2)}) collective-permute-start(bf16[4,32,2048]{2,1,0:T(8,128)(2,1)S(1)} %collective-permute-done.3.rest_2_), channel_id=1, source_target_pairs={{0,16},{16,32},{32,48},{48,64},{64,80},{80,96},{96,112},{112,0},{8... | collective-permute-start | bytes 1572872 | tf_op jit(solution)/shard_map/ppermute | solution.py:149
  51.3 3.3 %collective-permute-start.9 = (bf16[4,32,2048]{2,1,0:T(8,128)(2,1)S(1)}, bf16[4,32,2048]{2,1,0:T(8,128)(2,1)}, u32[]{:S(2)}, u32[]{:S(2)}) collective-permute-start(bf16[4,32,2048]{2,1,0:T(8,128)(2,1)S(1)} %collective-permute-done.3.rest_2_), channel_id=1, source_target_pairs={{0,8},{8,0},{1,9},{9,1},{2,10},{10,2},{3,11},{11,3},{4,12},{12,4},... | collective-permute-start | bytes 1572872 | tf_op jit(solution)/shard_map/ppermute | solution.py:50
  54.6 4.7 %collective-permute-start.5 = (bf16[4,32,2048]{2,1,0:T(8,128)(2,1)}, bf16[4,32,2048]{2,1,0:T(8,128)(2,1)}, u32[]{:S(2)}, u32[]{:S(2)}) collective-permute-start(bf16[4,32,2048]{2,1,0:T(8,128)(2,1)} %collective-permute-done.4.rest_6_), channel_id=1, source_target_pairs={{0,16},{16,32},{32,48},{48,64},{64,80},{80,96},{96,112},{112,0},{8... | collective-permute-start | bytes 1572872 | tf_op jit(solution)/shard_map/ppermute | solution.py:149
  59.3 2.3 %collective-permute-start.12 = (bf16[4,32,2048]{2,1,0:T(8,128)(2,1)}, bf16[4,32,2048]{2,1,0:T(8,128)(2,1)}, u32[]{:S(2)}, u32[]{:S(2)}) collective-permute-start(bf16[4,32,2048]{2,1,0:T(8,128)(2,1)} %collective-permute-done.4.rest_6_), channel_id=1, source_target_pairs={{0,8},{8,0},{1,9},{9,1},{2,10},{10,2},{3,11},{11,3},{4,12},{12,4},... | collective-permute-start | bytes 1572872 | tf_op jit(solution)/shard_map/ppermute | solution.py:50
  61.6 4.9 %collective-permute-start.13 = (bf16[4,32,2048]{2,1,0:T(8,128)(2,1)}, bf16[4,32,2048]{2,1,0:T(8,128)(2,1)}, u32[]{:S(2)}, u32[]{:S(2)}) collective-permute-start(bf16[4,32,2048]{2,1,0:T(8,128)(2,1)} %collective-permute-done.10.rest_4_), channel_id=1, source_target_pairs={{0,16},{16,32},{32,48},{48,64},{64,80},{80,96},{96,112},{112,0},{8... | collective-permute-start | bytes 1572872 | tf_op jit(solution)/shard_map/ppermute | solution.py:149
  69.5 3.7 %collective-permute-start.6 = (bf16[4,32,2048]{2,1,0:T(8,128)(2,1)}, bf16[4,32,2048]{2,1,0:T(8,128)(2,1)S(1)}, u32[]{:S(2)}, u32[]{:S(2)}) collective-permute-start(bf16[4,32,2048]{2,1,0:T(8,128)(2,1)} %collective-permute-done.5.rest_10_), channel_id=1, source_target_pairs={{0,16},{16,32},{32,48},{48,64},{64,80},{80,96},{96,112},{112,0},{8... | collective-permute-start | bytes 1572872 | tf_op jit(solution)/shard_map/ppermute | solution.py:149
  73.1 4.7 %collective-permute-start.16 = (bf16[4,32,2048]{2,1,0:T(8,128)(2,1)}, bf16[4,32,2048]{2,1,0:T(8,128)(2,1)S(1)}, u32[]{:S(2)}, u32[]{:S(2)}) collective-permute-start(bf16[4,32,2048]{2,1,0:T(8,128)(2,1)} %collective-permute-done.13.rest_8_), channel_id=1, source_target_pairs={{0,16},{16,32},{32,48},{48,64},{64,80},{80,96},{96,112},{112,0},{8... | collective-permute-start | bytes 1572872 | tf_op jit(solution)/shard_map/ppermute | solution.py:149
  79.9 4.8 %collective-permute-start.15 = (bf16[4,32,2048]{2,1,0:T(8,128)(2,1)}, bf16[4,32,2048]{2,1,0:T(8,128)(2,1)S(1)}, u32[]{:S(2)}, u32[]{:S(2)}) collective-permute-start(bf16[4,32,2048]{2,1,0:T(8,128)(2,1)} %collective-permute-done.5.rest_10_), channel_id=1, source_target_pairs={{0,8},{8,0},{1,9},{9,1},{2,10},{10,2},{3,11},{11,3},{4,12},{12,4},... | collective-permute-start | bytes 1572872 | tf_op jit(solution)/shard_map/ppermute | solution.py:50
  86.7 2.4 %collective-permute-start.18 = (bf16[4,32,2048]{2,1,0:T(8,128)(2,1)S(1)}, bf16[4,32,2048]{2,1,0:T(8,128)(2,1)S(1)}, u32[]{:S(2)}, u32[]{:S(2)}) collective-permute-start(bf16[4,32,2048]{2,1,0:T(8,128)(2,1)S(1)} %collective-permute-done.6.rest_14_), channel_id=1, source_target_pairs={{0,8},{8,0},{1,9},{9,1},{2,10},{10,2},{3,11},{11,3},{4,12},{12,4},... | collective-permute-start | bytes 1572872 | tf_op jit(solution)/shard_map/ppermute | solution.py:50
  93.1 10.1 %forward.1 = (f32[320,2048]{1,0:T(8,128)}, bf16[320,1024]{1,0:T(8,128)(2,1)}, bf16[8,32,1024]{2,1,0:T(8,128)(2,1)}) custom-call(s32[3]{0:T(128)} %compare_select_fusion.1.where, bf16[320,1024]{1,0:T(8,128)(2,1)} %bitcast.38, bf16[96,320]{1,0:T(8,128)(2,1)} %pad_maximum_fusion.4.mix_ref, bf16[4,32,2048]{2,1,0:T(8,128)(2,1)} %copy-done.2, ...), custom_call_target="tpu_custom_call" | custom-call | tf_op jit(solution)/shard_map/forward/pallas_call | solution.py:242
  103.2 18.7 %all_to_all.20 = bf16[8,32,1024]{2,1,0:T(8,128)(2,1)S(1)} all-to-all(bf16[8,32,1024]{2,1,0:T(8,128)(2,1)} %get-tuple-element.24), channel_id=1, replica_groups=mesh['a'=2,'b'=2,'y'=8,'c'=2,'x'=4,'zh'=2] {'x','b'}, dimensions={0} | all-to-all | bytes 1048576 | tf_op jit(solution)/shard_map/all_to_all | solution.py:261
  126.3 13.9 %all-to-all-start.2 = ((f32[64,8,128]{2,1,0:T(8,128)}), f32[64,8,128]{2,1,0:T(8,128)S(1)}, u32[]{:S(2)}, u32[]{:S(2)}) async-start(f32[64,8,128]{2,1,0:T(8,128)} %broadcast_in_dim.35), calls=%async_computation.2 | async-start | bytes 524288 | tf_op jit(solution)/shard_map/all_to_all | solution.py:161
  141.1 10.6 %backward.1 = bf16[8,48,1024]{2,1,0:T(8,128)(2,1)} custom-call(s32[3]{0:T(128)} %compare_select_fusion.1.where, bf16[320,1024]{1,0:T(8,128)(2,1)} %get-tuple-element.32.dy_ref, f32[320,2048]{1,0:T(8,128)} %get-tuple-element.27.hid_in, f32[320,1]{1,0:T(8,128)} %broadcast_in_dim.67.grad_logit, f32[1,1024]{1,0:T(1,128)} %bitcast.47, ...), custom_call_target="tpu_custom_call" | custom-call | tf_op jit(solution)/shard_map/backward/pallas_call | solution.py:285
  151.7 2.7 %all-to-all-done.2 = f32[64,8,128]{2,1,0:T(8,128)S(1)} async-done(((f32[64,8,128]{2,1,0:T(8,128)}), f32[64,8,128]{2,1,0:T(8,128)S(1)}, u32[]{:S(2)}, u32[]{:S(2)}) %all-to-all-start.2) | async-done | bytes 262176 | tf_op jit(solution)/shard_map/all_to_all | solution.py:161
  155.3 3.5 %all-to-all-start.3 = ((bf16[8,48,1024]{2,1,0:T(8,128)(2,1)}), bf16[8,48,1024]{2,1,0:T(8,128)(2,1)S(1)}, u32[]{:S(2)}, u32[]{:S(2)}) async-start(bf16[8,48,1024]{2,1,0:T(8,128)(2,1)} %broadcast_dynamic-update-slice_fusion), calls=%async_computation.3 | async-start | bytes 1572864 | tf_op jit(solution)/shard_map/all_to_all | solution.py:302
  161.6 3.0 %collective-permute-done.19 = f32[4,1024]{1,0:T(4,128)S(1)} collective-permute-done((f32[4,1024]{1,0:T(4,128)S(1)}, f32[4,1024]{1,0:T(4,128)S(1)}, u32[]{:S(2)}, u32[]{:S(2)}) %collective-permute-start.19) | collective-permute-done | bytes 16416 | tf_op jit(solution)/shard_map/ppermute | solution.py:318
  165.5 6.0 %all-to-all-done.3 = bf16[8,48,1024]{2,1,0:T(8,128)(2,1)S(1)} async-done(((bf16[8,48,1024]{2,1,0:T(8,128)(2,1)}), bf16[8,48,1024]{2,1,0:T(8,128)(2,1)S(1)}, u32[]{:S(2)}, u32[]{:S(2)}) %all-to-all-start.3) | async-done | bytes 786464 | tf_op jit(solution)/shard_map/all_to_all | solution.py:302
  (106 shorter events, 33.7 us)
Async XLA Ops:
  0.6 13.8 %collective-permute-start.7 = (bf16[4,1024]{1,0:T(4,128)(2,1)}, bf16[4,1024]{1,0:T(4,128)(2,1)S(1)}, u32[]{:S(2)}, u32[]{:S(2)}) collective-permute-start(bf16[4,1024]{1,0:T(4,128)(2,1)} %param.13), channel_id=1, source_target_pairs={{0,8},{8,16},{16,24},{24,32},{32,40},{40,48},{48,56},{56,64},{64,7... | collective-permute-start | bytes 24584 | tf_op jit(solution)/shard_map/ppermute | solution.py:191
  6.1 8.4 %collective-permute-start = (bf16[32,2048]{1,0:T(8,128)(2,1)S(1)}, bf16[32,2048]{1,0:T(8,128)(2,1)S(1)}, u32[]{:S(2)}, u32[]{:S(2)}) collective-permute-start(bf16[32,2048]{1,0:T(8,128)(2,1)S(1)} %get-tuple-element.36), channel_id=1, source_target_pairs={{0,8},{8,0},{1,9},{9,1},{2,10},{10,2},{3,11},{11,3},{4,12},{12,4},... | collective-permute-start | bytes 393224 | tf_op jit(solution)/shard_map/ppermute | solution.py:50
  14.6 17.9 %collective-permute-start.1 = (bf16[2,32,2048]{2,1,0:T(8,128)(2,1)S(1)}, bf16[2,32,2048]{2,1,0:T(8,128)(2,1)S(1)}, u32[]{:S(2)}, u32[]{:S(2)}) collective-permute-start(bf16[2,32,2048]{2,1,0:T(8,128)(2,1)S(1)} %pad_maximum_fusion.1), channel_id=1, source_target_pairs={{0,0},{128,256},{256,1},{384,257},{1,128},{129,384},{257,129},{385... | collective-permute-start | bytes 786440 | tf_op jit(solution)/shard_map/ppermute | solution.py:143
  21.0 11.4 %collective-permute-start.2 = (bf16[2,32,2048]{2,1,0:T(8,128)(2,1)S(1)}, bf16[2,32,2048]{2,1,0:T(8,128)(2,1)S(1)}, u32[]{:S(2)}, u32[]{:S(2)}) collective-permute-start(bf16[2,32,2048]{2,1,0:T(8,128)(2,1)S(1)} %pad_maximum_fusion.1), channel_id=1, source_target_pairs={{0,256},{128,1},{256,257},{384,0},{1,384},{129,129},{257,385},{385... | collective-permute-start | bytes 786440 | tf_op jit(solution)/shard_map/ppermute | solution.py:143
  24.0 44.4 %all-to-all-start = ((bf16[8,48,1152]{2,1,0:T(8,128)(2,1)}), bf16[8,48,1152]{2,1,0:T(8,128)(2,1)S(1)}, u32[]{:S(2)}, u32[]{:S(2)}) async-start(bf16[8,48,1152]{2,1,0:T(8,128)(2,1)} %pad_maximum_fusion), calls=%async_computation | async-start | bytes 1769472 | tf_op jit(solution)/shard_map/all_to_all | solution.py:213
  32.5 36.4 %copy-start.2 = (bf16[4,32,2048]{2,1,0:T(8,128)(2,1)}, bf16[4,32,2048]{2,1,0:T(8,128)(2,1)S(1)}, u32[]{:S(2)}) copy-start(bf16[4,32,2048]{2,1,0:T(8,128)(2,1)S(1)} %constant_dynamic-update-slice_fusion.rest_0_) | copy-start | bytes 1572868
  32.5 10.3 %collective-permute-start.3 = (bf16[4,32,2048]{2,1,0:T(8,128)(2,1)S(1)}, bf16[4,32,2048]{2,1,0:T(8,128)(2,1)S(1)}, u32[]{:S(2)}, u32[]{:S(2)}) collective-permute-start(bf16[4,32,2048]{2,1,0:T(8,128)(2,1)S(1)} %constant_dynamic-update-slice_fusion.rest_0_), channel_id=1, source_target_pairs={{0,16},{16,32},{32,48},{48,64},{64,80},{80,96},{96,112},{112,0},{8... | collective-permute-start | bytes 1572872 | tf_op jit(solution)/shard_map/ppermute | solution.py:149
  36.7 11.4 %collective-permute-start.8 = (bf16[4,32,2048]{2,1,0:T(8,128)(2,1)S(1)}, bf16[4,32,2048]{2,1,0:T(8,128)(2,1)S(1)}, u32[]{:S(2)}, u32[]{:S(2)}) collective-permute-start(bf16[4,32,2048]{2,1,0:T(8,128)(2,1)S(1)} %constant_dynamic-update-slice_fusion.rest_0_), channel_id=1, source_target_pairs={{0,8},{8,0},{1,9},{9,1},{2,10},{10,2},{3,11},{11,3},{4,12},{12,4},... | collective-permute-start | bytes 1572872 | tf_op jit(solution)/shard_map/ppermute | solution.py:50
  42.8 11.8 %collective-permute-start.4 = (bf16[4,32,2048]{2,1,0:T(8,128)(2,1)S(1)}, bf16[4,32,2048]{2,1,0:T(8,128)(2,1)}, u32[]{:S(2)}, u32[]{:S(2)}) collective-permute-start(bf16[4,32,2048]{2,1,0:T(8,128)(2,1)S(1)} %collective-permute-done.3.rest_2_), channel_id=1, source_target_pairs={{0,16},{16,32},{32,48},{48,64},{64,80},{80,96},{96,112},{112,0},{8... | collective-permute-start | bytes 1572872 | tf_op jit(solution)/shard_map/ppermute | solution.py:149
  48.1 13.5 %collective-permute-start.10 = (bf16[4,32,2048]{2,1,0:T(8,128)(2,1)S(1)}, bf16[4,32,2048]{2,1,0:T(8,128)(2,1)}, u32[]{:S(2)}, u32[]{:S(2)}) collective-permute-start(bf16[4,32,2048]{2,1,0:T(8,128)(2,1)S(1)} %collective-permute-done.8.rest_1_), channel_id=1, source_target_pairs={{0,16},{16,32},{32,48},{48,64},{64,80},{80,96},{96,112},{112,0},{8... | collective-permute-start | bytes 1572872 | tf_op jit(solution)/shard_map/ppermute | solution.py:149
  51.3 33.4 %collective-permute-start.9 = (bf16[4,32,2048]{2,1,0:T(8,128)(2,1)S(1)}, bf16[4,32,2048]{2,1,0:T(8,128)(2,1)}, u32[]{:S(2)}, u32[]{:S(2)}) collective-permute-start(bf16[4,32,2048]{2,1,0:T(8,128)(2,1)S(1)} %collective-permute-done.3.rest_2_), channel_id=1, source_target_pairs={{0,8},{8,0},{1,9},{9,1},{2,10},{10,2},{3,11},{11,3},{4,12},{12,4},... | collective-permute-start | bytes 1572872 | tf_op jit(solution)/shard_map/ppermute | solution.py:50
  54.6 14.9 %collective-permute-start.5 = (bf16[4,32,2048]{2,1,0:T(8,128)(2,1)}, bf16[4,32,2048]{2,1,0:T(8,128)(2,1)}, u32[]{:S(2)}, u32[]{:S(2)}) collective-permute-start(bf16[4,32,2048]{2,1,0:T(8,128)(2,1)} %collective-permute-done.4.rest_6_), channel_id=1, source_target_pairs={{0,16},{16,32},{32,48},{48,64},{64,80},{80,96},{96,112},{112,0},{8... | collective-permute-start | bytes 1572872 | tf_op jit(solution)/shard_map/ppermute | solution.py:149
  59.3 27.4 %collective-permute-start.12 = (bf16[4,32,2048]{2,1,0:T(8,128)(2,1)}, bf16[4,32,2048]{2,1,0:T(8,128)(2,1)}, u32[]{:S(2)}, u32[]{:S(2)}) collective-permute-start(bf16[4,32,2048]{2,1,0:T(8,128)(2,1)} %collective-permute-done.4.rest_6_), channel_id=1, source_target_pairs={{0,8},{8,0},{1,9},{9,1},{2,10},{10,2},{3,11},{11,3},{4,12},{12,4},... | collective-permute-start | bytes 1572872 | tf_op jit(solution)/shard_map/ppermute | solution.py:50
  61.6 11.5 %collective-permute-start.13 = (bf16[4,32,2048]{2,1,0:T(8,128)(2,1)}, bf16[4,32,2048]{2,1,0:T(8,128)(2,1)}, u32[]{:S(2)}, u32[]{:S(2)}) collective-permute-start(bf16[4,32,2048]{2,1,0:T(8,128)(2,1)} %collective-permute-done.10.rest_4_), channel_id=1, source_target_pairs={{0,16},{16,32},{32,48},{48,64},{64,80},{80,96},{96,112},{112,0},{8... | collective-permute-start | bytes 1572872 | tf_op jit(solution)/shard_map/ppermute | solution.py:149
  66.5 24.6 %collective-permute-start.11 = (bf16[4,32,2048]{2,1,0:T(8,128)(2,1)}, bf16[4,32,2048]{2,1,0:T(8,128)(2,1)}, u32[]{:S(2)}, u32[]{:S(2)}) collective-permute-start(bf16[4,32,2048]{2,1,0:T(8,128)(2,1)} %collective-permute-done.10.rest_4_), channel_id=1, source_target_pairs={{0,8},{8,0},{1,9},{9,1},{2,10},{10,2},{3,11},{11,3},{4,12},{12,4},... | collective-permute-start | bytes 1572872 | tf_op jit(solution)/shard_map/ppermute | solution.py:50
  69.5 10.4 %collective-permute-start.6 = (bf16[4,32,2048]{2,1,0:T(8,128)(2,1)}, bf16[4,32,2048]{2,1,0:T(8,128)(2,1)S(1)}, u32[]{:S(2)}, u32[]{:S(2)}) collective-permute-start(bf16[4,32,2048]{2,1,0:T(8,128)(2,1)} %collective-permute-done.5.rest_10_), channel_id=1, source_target_pairs={{0,16},{16,32},{32,48},{48,64},{64,80},{80,96},{96,112},{112,0},{8... | collective-permute-start | bytes 1572872 | tf_op jit(solution)/shard_map/ppermute | solution.py:149
  73.1 16.0 %collective-permute-start.16 = (bf16[4,32,2048]{2,1,0:T(8,128)(2,1)}, bf16[4,32,2048]{2,1,0:T(8,128)(2,1)S(1)}, u32[]{:S(2)}, u32[]{:S(2)}) collective-permute-start(bf16[4,32,2048]{2,1,0:T(8,128)(2,1)} %collective-permute-done.13.rest_8_), channel_id=1, source_target_pairs={{0,16},{16,32},{32,48},{48,64},{64,80},{80,96},{96,112},{112,0},{8... | collective-permute-start | bytes 1572872 | tf_op jit(solution)/shard_map/ppermute | solution.py:149
  79.9 11.2 %collective-permute-start.15 = (bf16[4,32,2048]{2,1,0:T(8,128)(2,1)}, bf16[4,32,2048]{2,1,0:T(8,128)(2,1)S(1)}, u32[]{:S(2)}, u32[]{:S(2)}) collective-permute-start(bf16[4,32,2048]{2,1,0:T(8,128)(2,1)} %collective-permute-done.5.rest_10_), channel_id=1, source_target_pairs={{0,8},{8,0},{1,9},{9,1},{2,10},{10,2},{3,11},{11,3},{4,12},{12,4},... | collective-permute-start | bytes 1572872 | tf_op jit(solution)/shard_map/ppermute | solution.py:50
  84.7 6.3 %collective-permute-start.14 = (bf16[4,32,2048]{2,1,0:T(8,128)(2,1)}, bf16[4,32,2048]{2,1,0:T(8,128)(2,1)S(1)}, u32[]{:S(2)}, u32[]{:S(2)}) collective-permute-start(bf16[4,32,2048]{2,1,0:T(8,128)(2,1)} %collective-permute-done.13.rest_8_), channel_id=1, source_target_pairs={{0,8},{8,0},{1,9},{9,1},{2,10},{10,2},{3,11},{11,3},{4,12},{12,4},... | collective-permute-start | bytes 1572872 | tf_op jit(solution)/shard_map/ppermute | solution.py:50
  86.7 4.4 %collective-permute-start.18 = (bf16[4,32,2048]{2,1,0:T(8,128)(2,1)S(1)}, bf16[4,32,2048]{2,1,0:T(8,128)(2,1)S(1)}, u32[]{:S(2)}, u32[]{:S(2)}) collective-permute-start(bf16[4,32,2048]{2,1,0:T(8,128)(2,1)S(1)} %collective-permute-done.6.rest_14_), channel_id=1, source_target_pairs={{0,8},{8,0},{1,9},{9,1},{2,10},{10,2},{3,11},{11,3},{4,12},{12,4},... | collective-permute-start | bytes 1572872 | tf_op jit(solution)/shard_map/ppermute | solution.py:50
  89.1 3.9 %collective-permute-start.17 = (bf16[4,32,2048]{2,1,0:T(8,128)(2,1)S(1)}, bf16[4,32,2048]{2,1,0:T(8,128)(2,1)}, u32[]{:S(2)}, u32[]{:S(2)}) collective-permute-start(bf16[4,32,2048]{2,1,0:T(8,128)(2,1)S(1)} %collective-permute-done.16.rest_12_), channel_id=1, source_target_pairs={{0,8},{8,0},{1,9},{9,1},{2,10},{10,2},{3,11},{11,3},{4,12},{12,4},... | collective-permute-start | bytes 1572872 | tf_op jit(solution)/shard_map/ppermute | solution.py:50
  126.3 28.1 %all-to-all-start.2 = ((f32[64,8,128]{2,1,0:T(8,128)}), f32[64,8,128]{2,1,0:T(8,128)S(1)}, u32[]{:S(2)}, u32[]{:S(2)}) async-start(f32[64,8,128]{2,1,0:T(8,128)} %broadcast_in_dim.35), calls=%async_computation.2 | async-start | bytes 524288 | tf_op jit(solution)/shard_map/all_to_all | solution.py:161
  155.3 16.2 %all-to-all-start.3 = ((bf16[8,48,1024]{2,1,0:T(8,128)(2,1)}), bf16[8,48,1024]{2,1,0:T(8,128)(2,1)S(1)}, u32[]{:S(2)}, u32[]{:S(2)}) async-start(bf16[8,48,1024]{2,1,0:T(8,128)(2,1)} %broadcast_dynamic-update-slice_fusion), calls=%async_computation.3 | async-start | bytes 1572864 | tf_op jit(solution)/shard_map/all_to_all | solution.py:302
  159.3 5.4 %collective-permute-start.19 = (f32[4,1024]{1,0:T(4,128)S(1)}, f32[4,1024]{1,0:T(4,128)S(1)}, u32[]{:S(2)}, u32[]{:S(2)}) collective-permute-start(f32[4,1024]{1,0:T(4,128)S(1)} %constant_dynamic-slice_fusion.1), channel_id=1, source_target_pairs={{8,0},{16,8},{24,16},{32,24},{40,32},{48,40},{56,48},{64,56},{72,6... | collective-permute-start | bytes 49160 | tf_op jit(solution)/shard_map/ppermute | solution.py:318
  (12 other events, 135.9 us)

commit v2 on v1

--- a/solution.py
+++ b/solution.py
@@ -78,8 +78,8 @@
     refs = rest[:count]
     hid_out, out_ref, part_ref, win, wout, act, hid, sems, hid_sems = rest[count:]
     start_copies(where, parts, refs, win, sems.at[0], 0)
+    wait_all(win, sems.at[0])
     start_copies(where, parts, refs, wout, sems.at[1], 1)
-    wait_all(win, sems.at[0])
     leaving = []
     for n in range(4):
         at = slice(n * 512, n * 512 + 512)
@@ -112,18 +112,15 @@
     return 0.5 * (1.0 + bent) + 0.5 * hidden * (1.0 - bent * bent) * inner
 
 
-def backward_kernel(parts, count, where, dy_ref, hid_in, grad_logit, router_row, *rest):
-    refs, (back_ref, win, wout, dhid, hid, sems, hid_sem) = rest[:count], rest[count:]
+def backward_kernel(parts, count, where, dy_ref, hid_ref, grad_logit, router_row, *rest):
+    refs, (back_ref, win, wout, dhid, sems) = rest[:count], rest[count:]
     start_copies(where, parts, refs, wout, sems.at[1], 1)
-    entering = pltpu.make_async_copy(hid_in, hid, hid_sem)
-    entering.start()
+    wait_all(wout, sems.at[1])
     start_copies(where, parts, refs, win, sems.at[0], 0)
-    wait_all(wout, sems.at[1])
-    entering.wait()
     for n in range(4):
         at = slice(n * 512, n * 512 + 512)
         grad = jnp.dot(dy_ref[...], wout[:, at], preferred_element_type=jnp.float32)
-        dhid[:, at] = (grad * gelu_slope(hid[:, at])).astype(jnp.bfloat16)
+        dhid[:, at] = (grad * gelu_slope(hid_ref[:, at])).astype(jnp.bfloat16)
     wait_all(win, sems.at[0])
     members, _, width = back_ref.shape
     capacity = dhid.shape[0] // members
@@ -151,7 +148,9 @@
             arrays.append(moved)
             parts.append((step, False, n == 1))
             if step == 4:
-                moved, settled = lax.optimization_barrier((moved, settle()))
+                moved, settled, arrays[-2] = lax.optimization_barrier(
+                    (moved, settle(), arrays[-2])
+                )
             arrays.append(swap_cores(moved))
             parts.append((step, True, n == 0))
     return arrays, parts, settled
@@ -285,15 +284,10 @@
     back = pl.pallas_call(
         functools.partial(backward_kernel, parts, len(arrays)),
         out_shape=jax.ShapeDtypeStruct((experts, capacity + 8, width), bf16),
-        in_specs=[SMEM, VMEM, ANY, VMEM, VMEM] + [ANY] * len(arrays),
+        in_specs=[SMEM, VMEM, VMEM, VMEM, VMEM] + [ANY] * len(arrays),
         out_specs=VMEM,
         scratch_shapes=weight_scratch
-        + [
-            pltpu.VMEM((rows, hidden_width), bf16),
-            pltpu.VMEM((rows, hidden_width), f32),
-            pltpu.SemaphoreType.DMA((2,)),
-            pltpu.SemaphoreType.DMA,
-        ],
+        + [pltpu.VMEM((rows, hidden_width), bf16), pltpu.SemaphoreType.DMA((2,))],
         name="backward",
     )(where, grad_out, hidden, grad_logit[:, None], router_row, *arrays)
     tail = jnp.concatenate([high, middle, low, jnp.zeros((5, width), bf16)], axis=0)

time: 175 us -> 178 us (1.017)
  waiting for transfers between devices: 20.7 us -> 26.3 us
    ppermute x7, waiting for transfers between devices: 5.41 us -> 8.38 us  [gathered_weights(): moved = lax.ppermute(chunks[n], ('y', 'c'), ring_route())]
    ppermute x7, starting transfers between devices: 29.3 us -> 27 us  [gathered_weights(): moved = lax.ppermute(chunks[n], ('y', 'c'), ring_route())]
    pallas_call x1, Pallas kernels: 10.1 us -> 12.2 us  [layer(): pl.pallas_call(functools.partial(forward_kernel, parts, len(arrays)), out...]
  transfers between devices with their start and end apart: 23 -> 23, of which waited for: 7 -> 9; matrix products, arithmetic and copies ran while one was open for 5% -> 5% of each run, Pallas kernels for 6% -> 5%
where the time goes in v2:
time: 178 us; the launch traced here: 177 us
  starting transfers between devices  92.5 us (52%)
  waiting for transfers between devices  26.3 us (15%)
  Pallas kernels  21.4 us (12%)
  blocking collectives  18.3 us (10%)
  matrix products  7.06 us (4%)
  other arithmetic  6.78 us (4%)
  local copies, waits for them, and re-layouts  3.47 us (2%)
    ppermute x9, starting transfers between devices, swap_cores(): return lax.ppermute(block, 'c', [(0, 1), (1, 0)])  27.1 us
    ppermute x7, starting transfers between devices, gathered_weights(): moved = lax.ppermute(chunks[n], ('y', 'c'), ring_route())  27 us
    all_to_all x1, blocking collectives, layer(): shared = lax.all_to_all(part, GROUP, 0, 0, tiled=True)  18.3 us
    all_to_all x1, starting transfers between devices, share(): lax.all_to_all(jnp.broadcast_to(block[None], (count,) + block.shape), axe...  14.4 us
    pallas_call x1, Pallas kernels, layer(): pl.pallas_call(functools.partial(forward_kernel, parts, len(arrays)), out...  12.2 us
    pallas_call x1, Pallas kernels, layer(): pl.pallas_call(functools.partial(backward_kernel, parts, len(arrays)), ou...  9.16 us
    ppermute x2, starting transfers between devices, gathered_weights(): lax.ppermute(pair, DEEP, depth_round(n))  8.41 us
    ppermute x7, waiting for transfers between devices, gathered_weights(): moved = lax.ppermute(chunks[n], ('y', 'c'), ring_route())  8.38 us
  transfers between devices with their start and end apart: 23, of which 9 were waited for; matrix products, arithmetic and copies ran while one was open for 5% of the time, Pallas kernels for 5%

profile of v2, /device:TPU:1, one launch (start us, length us, event | category | flops | bytes accessed | tf_op | source)
XLA Modules:
  0.0 176.9 jit_solution(16176870053329465753)
XLA Ops:
  0.6 4.6 %collective-permute-start.7 = (bf16[4,1024]{1,0:T(4,128)(2,1)}, bf16[4,1024]{1,0:T(4,128)(2,1)S(1)}, u32[]{:S(2)}, u32[]{:S(2)}) collective-permute-start(bf16[4,1024]{1,0:T(4,128)(2,1)} %param.13), channel_id=1, source_target_pairs={{0,8},{8,16},{16,24},{24,32},{32,40},{40,48},{48,56},{56,64},{64,7... | collective-permute-start | bytes 24584 | tf_op jit(solution)/shard_map/ppermute | solution.py:190
  6.1 6.1 %collective-permute-start = (bf16[32,2048]{1,0:T(8,128)(2,1)S(1)}, bf16[32,2048]{1,0:T(8,128)(2,1)S(1)}, u32[]{:S(2)}, u32[]{:S(2)}) collective-permute-start(bf16[32,2048]{1,0:T(8,128)(2,1)S(1)} %get-tuple-element.38), channel_id=1, source_target_pairs={{0,8},{8,0},{1,9},{9,1},{2,10},{10,2},{3,11},{11,3},{4,12},{12,4},... | collective-permute-start | bytes 393224 | tf_op jit(solution)/shard_map/ppermute | solution.py:50
  14.6 6.5 %collective-permute-start.1 = (bf16[2,32,2048]{2,1,0:T(8,128)(2,1)S(1)}, bf16[2,32,2048]{2,1,0:T(8,128)(2,1)S(1)}, u32[]{:S(2)}, u32[]{:S(2)}) collective-permute-start(bf16[2,32,2048]{2,1,0:T(8,128)(2,1)S(1)} %pad_maximum_fusion.1), channel_id=1, source_target_pairs={{0,0},{128,256},{256,1},{384,257},{1,128},{129,384},{257,129},{385... | collective-permute-start | bytes 786440 | tf_op jit(solution)/shard_map/ppermute | solution.py:140
  24.0 5.3 %all-to-all-start = ((bf16[8,48,1152]{2,1,0:T(8,128)(2,1)}), bf16[8,48,1152]{2,1,0:T(8,128)(2,1)S(1)}, u32[]{:S(2)}, u32[]{:S(2)}) async-start(bf16[8,48,1152]{2,1,0:T(8,128)(2,1)} %pad_maximum_fusion), calls=%async_computation | async-start | bytes 1769472 | tf_op jit(solution)/shard_map/all_to_all | solution.py:212
  29.3 3.1 %collective-permute-done.1 = bf16[2,32,2048]{2,1,0:T(8,128)(2,1)S(1)} collective-permute-done((bf16[2,32,2048]{2,1,0:T(8,128)(2,1)S(1)}, bf16[2,32,2048]{2,1,0:T(8,128)(2,1)S(1)}, u32[]{:S(2)}, u32[]{:S(2)}) %collective-permute-start.1) | collective-permute-done | bytes 262176 | tf_op jit(solution)/shard_map/ppermute | solution.py:140
  35.0 4.2 %collective-permute-start.3 = (bf16[4,32,2048]{2,1,0:T(8,128)(2,1)S(1)}, bf16[4,32,2048]{2,1,0:T(8,128)(2,1)S(1)}, u32[]{:S(2)}, u32[]{:S(2)}) collective-permute-start(bf16[4,32,2048]{2,1,0:T(8,128)(2,1)S(1)} %constant_dynamic-update-slice_fusion.rest_0_), channel_id=1, source_target_pairs={{0,16},{16,32},{32,48},{48,64},{64,80},{80,96},{96,112},{112,0},{8... | collective-permute-start | bytes 1572872 | tf_op jit(solution)/shard_map/ppermute | solution.py:146
  39.2 3.0 %collective-permute-start.9 = (bf16[4,32,2048]{2,1,0:T(8,128)(2,1)S(1)}, bf16[4,32,2048]{2,1,0:T(8,128)(2,1)}, u32[]{:S(2)}, u32[]{:S(2)}) collective-permute-start(bf16[4,32,2048]{2,1,0:T(8,128)(2,1)S(1)} %collective-permute-done.8.rest_1_), channel_id=1, source_target_pairs={{0,16},{16,32},{32,48},{48,64},{64,80},{80,96},{96,112},{112,0},{8... | collective-permute-start | bytes 1572872 | tf_op jit(solution)/shard_map/ppermute | solution.py:146
  42.2 3.1 %collective-permute-done.3.rest_2_ = bf16[4,32,2048]{2,1,0:T(8,128)(2,1)S(1)} collective-permute-done((bf16[4,32,2048]{2,1,0:T(8,128)(2,1)S(1)}, bf16[4,32,2048]{2,1,0:T(8,128)(2,1)S(1)}, u32[]{:S(2)}, u32[]{:S(2)}) %collective-permute-start.3) | collective-permute-done | bytes 524320 | tf_op jit(solution)/shard_map/ppermute | solution.py:146
  45.3 5.0 %collective-permute-start.4 = (bf16[4,32,2048]{2,1,0:T(8,128)(2,1)S(1)}, bf16[4,32,2048]{2,1,0:T(8,128)(2,1)}, u32[]{:S(2)}, u32[]{:S(2)}) collective-permute-start(bf16[4,32,2048]{2,1,0:T(8,128)(2,1)S(1)} %collective-permute-done.3.rest_2_), channel_id=1, source_target_pairs={{0,16},{16,32},{32,48},{48,64},{64,80},{80,96},{96,112},{112,0},{8... | collective-permute-start | bytes 1572872 | tf_op jit(solution)/shard_map/ppermute | solution.py:146
  50.9 5.1 %collective-permute-start.10 = (bf16[4,32,2048]{2,1,0:T(8,128)(2,1)}, bf16[4,32,2048]{2,1,0:T(8,128)(2,1)}, u32[]{:S(2)}, u32[]{:S(2)}) collective-permute-start(bf16[4,32,2048]{2,1,0:T(8,128)(2,1)} %collective-permute-done.9.rest_4_), channel_id=1, source_target_pairs={{0,16},{16,32},{32,48},{48,64},{64,80},{80,96},{96,112},{112,0},{8... | collective-permute-start | bytes 1572872 | tf_op jit(solution)/shard_map/ppermute | solution.py:146
  59.1 3.8 %collective-permute-start.5 = (bf16[4,32,2048]{2,1,0:T(8,128)(2,1)}, bf16[4,32,2048]{2,1,0:T(8,128)(2,1)}, u32[]{:S(2)}, u32[]{:S(2)}) collective-permute-start(bf16[4,32,2048]{2,1,0:T(8,128)(2,1)} %collective-permute-done.4.rest_6_), channel_id=1, source_target_pairs={{0,16},{16,32},{32,48},{48,64},{64,80},{80,96},{96,112},{112,0},{8... | collective-permute-start | bytes 1572872 | tf_op jit(solution)/shard_map/ppermute | solution.py:146
  67.8 3.0 %collective-permute-start.11 = (bf16[4,32,2048]{2,1,0:T(8,128)(2,1)}, bf16[4,32,2048]{2,1,0:T(8,128)(2,1)}, u32[]{:S(2)}, u32[]{:S(2)}) collective-permute-start(bf16[4,32,2048]{2,1,0:T(8,128)(2,1)} %collective-permute-done.10.rest_8_), channel_id=1, source_target_pairs={{0,16},{16,32},{32,48},{48,64},{64,80},{80,96},{96,112},{112,0},{8... | collective-permute-start | bytes 1572872 | tf_op jit(solution)/shard_map/ppermute | solution.py:146
  71.4 3.0 %collective-permute-start.6 = (bf16[4,32,2048]{2,1,0:T(8,128)(2,1)}, bf16[4,32,2048]{2,1,0:T(8,128)(2,1)S(1)}, u32[]{:S(2)}, u32[]{:S(2)}) collective-permute-start(bf16[4,32,2048]{2,1,0:T(8,128)(2,1)} %collective-permute-done.5.rest_10_), channel_id=1, source_target_pairs={{0,16},{16,32},{32,48},{48,64},{64,80},{80,96},{96,112},{112,0},{8... | collective-permute-start | bytes 1572872 | tf_op jit(solution)/shard_map/ppermute | solution.py:146
  74.3 3.9 %collective-permute-done.11.rest_12_ = bf16[4,32,2048]{2,1,0:T(8,128)(2,1)} collective-permute-done((bf16[4,32,2048]{2,1,0:T(8,128)(2,1)}, bf16[4,32,2048]{2,1,0:T(8,128)(2,1)}, u32[]{:S(2)}, u32[]{:S(2)}) %collective-permute-start.11) | collective-permute-done | bytes 524320 | tf_op jit(solution)/shard_map/ppermute | solution.py:146
  78.3 4.0 %collective-permute-start.12 = (bf16[4,32,2048]{2,1,0:T(8,128)(2,1)}, bf16[4,32,2048]{2,1,0:T(8,128)(2,1)S(1)}, u32[]{:S(2)}, u32[]{:S(2)}) collective-permute-start(bf16[4,32,2048]{2,1,0:T(8,128)(2,1)} %collective-permute-done.11.rest_12_), channel_id=1, source_target_pairs={{0,8},{8,0},{1,9},{9,1},{2,10},{10,2},{3,11},{11,3},{4,12},{12,4},... | collective-permute-start | bytes 1572872 | tf_op jit(solution)/shard_map/ppermute | solution.py:50
  83.8 4.0 %collective-permute-start.17 = (bf16[4,32,2048]{2,1,0:T(8,128)(2,1)}, bf16[4,32,2048]{2,1,0:T(8,128)(2,1)}, u32[]{:S(2)}, u32[]{:S(2)}) collective-permute-start(bf16[4,32,2048]{2,1,0:T(8,128)(2,1)} %collective-permute-done.5.rest_10_), channel_id=1, source_target_pairs={{0,8},{8,0},{1,9},{9,1},{2,10},{10,2},{3,11},{11,3},{4,12},{12,4},... | collective-permute-start | bytes 1572872 | tf_op jit(solution)/shard_map/ppermute | solution.py:50
  94.5 12.2 %forward.1 = (f32[320,2048]{1,0:T(8,128)}, bf16[320,1024]{1,0:T(8,128)(2,1)}, bf16[8,32,1024]{2,1,0:T(8,128)(2,1)}) custom-call(s32[3]{0:T(128)} %compare_select_fusion.1.where, bf16[320,1024]{1,0:T(8,128)(2,1)} %bitcast.38, bf16[96,320]{1,0:T(8,128)(2,1)} %pad_maximum_fusion.4.mix_ref, bf16[4,32,2048]{2,1,0:T(8,128)(2,1)} %copy-done.2, ...), custom_call_target="tpu_custom_call" | custom-call | tf_op jit(solution)/shard_map/forward/pallas_call | solution.py:241
  106.7 18.3 %all_to_all.20 = bf16[8,32,1024]{2,1,0:T(8,128)(2,1)S(1)} all-to-all(bf16[8,32,1024]{2,1,0:T(8,128)(2,1)} %get-tuple-element.26), channel_id=1, replica_groups=mesh['a'=2,'b'=2,'y'=8,'c'=2,'x'=4,'zh'=2] {'x','b'}, dimensions={0} | all-to-all | bytes 1048576 | tf_op jit(solution)/shard_map/all_to_all | solution.py:260
  129.2 14.4 %all-to-all-start.2 = ((f32[64,8,128]{2,1,0:T(8,128)}), f32[64,8,128]{2,1,0:T(8,128)S(1)}, u32[]{:S(2)}, u32[]{:S(2)}) async-start(f32[64,8,128]{2,1,0:T(8,128)} %broadcast_in_dim.35), calls=%async_computation.2 | async-start | bytes 524288 | tf_op jit(solution)/shard_map/all_to_all | solution.py:160
  144.5 9.2 %backward.1 = bf16[8,48,1024]{2,1,0:T(8,128)(2,1)} custom-call(s32[3]{0:T(128)} %compare_select_fusion.1.where, bf16[320,1024]{1,0:T(8,128)(2,1)} %get-tuple-element.34.dy_ref, f32[320,2048]{1,0:T(8,128)} %get-tuple-element.29.hid_ref, f32[320,1]{1,0:T(8,128)} %broadcast_in_dim.67.grad_logit, f32[1,1024]{1,0:T(1,128)} %bitcast.47, ...), custom_call_target="tpu_custom_call" | custom-call | tf_op jit(solution)/shard_map/backward/pallas_call | solution.py:284
  153.7 4.2 %all-to-all-done.2 = f32[64,8,128]{2,1,0:T(8,128)S(1)} async-done(((f32[64,8,128]{2,1,0:T(8,128)}), f32[64,8,128]{2,1,0:T(8,128)S(1)}, u32[]{:S(2)}, u32[]{:S(2)}) %all-to-all-start.2) | async-done | bytes 262176 | tf_op jit(solution)/shard_map/all_to_all | solution.py:160
  158.7 3.5 %all-to-all-start.3 = ((bf16[8,48,1024]{2,1,0:T(8,128)(2,1)}), bf16[8,48,1024]{2,1,0:T(8,128)(2,1)S(1)}, u32[]{:S(2)}, u32[]{:S(2)}) async-start(bf16[8,48,1024]{2,1,0:T(8,128)(2,1)} %broadcast_dynamic-update-slice_fusion), calls=%async_computation.3 | async-start | bytes 1572864 | tf_op jit(solution)/shard_map/all_to_all | solution.py:296
  165.1 3.0 %collective-permute-done.19 = f32[4,1024]{1,0:T(4,128)S(1)} collective-permute-done((f32[4,1024]{1,0:T(4,128)S(1)}, f32[4,1024]{1,0:T(4,128)S(1)}, u32[]{:S(2)}, u32[]{:S(2)}) %collective-permute-start.19) | collective-permute-done | bytes 16416 | tf_op jit(solution)/shard_map/ppermute | solution.py:312
  168.9 6.0 %all-to-all-done.3 = bf16[8,48,1024]{2,1,0:T(8,128)(2,1)S(1)} async-done(((bf16[8,48,1024]{2,1,0:T(8,128)(2,1)}), bf16[8,48,1024]{2,1,0:T(8,128)(2,1)S(1)}, u32[]{:S(2)}, u32[]{:S(2)}) %all-to-all-start.3) | async-done | bytes 786464 | tf_op jit(solution)/shard_map/all_to_all | solution.py:296
  (101 shorter events, 37.4 us)
Async XLA Ops:
  0.6 13.8 %collective-permute-start.7 = (bf16[4,1024]{1,0:T(4,128)(2,1)}, bf16[4,1024]{1,0:T(4,128)(2,1)S(1)}, u32[]{:S(2)}, u32[]{:S(2)}) collective-permute-start(bf16[4,1024]{1,0:T(4,128)(2,1)} %param.13), channel_id=1, source_target_pairs={{0,8},{8,16},{16,24},{24,32},{32,40},{40,48},{48,56},{56,64},{64,7... | collective-permute-start | bytes 24584 | tf_op jit(solution)/shard_map/ppermute | solution.py:190
  6.1 8.4 %collective-permute-start = (bf16[32,2048]{1,0:T(8,128)(2,1)S(1)}, bf16[32,2048]{1,0:T(8,128)(2,1)S(1)}, u32[]{:S(2)}, u32[]{:S(2)}) collective-permute-start(bf16[32,2048]{1,0:T(8,128)(2,1)S(1)} %get-tuple-element.38), channel_id=1, source_target_pairs={{0,8},{8,0},{1,9},{9,1},{2,10},{10,2},{3,11},{11,3},{4,12},{12,4},... | collective-permute-start | bytes 393224 | tf_op jit(solution)/shard_map/ppermute | solution.py:50
  14.6 17.9 %collective-permute-start.1 = (bf16[2,32,2048]{2,1,0:T(8,128)(2,1)S(1)}, bf16[2,32,2048]{2,1,0:T(8,128)(2,1)S(1)}, u32[]{:S(2)}, u32[]{:S(2)}) collective-permute-start(bf16[2,32,2048]{2,1,0:T(8,128)(2,1)S(1)} %pad_maximum_fusion.1), channel_id=1, source_target_pairs={{0,0},{128,256},{256,1},{384,257},{1,128},{129,384},{257,129},{385... | collective-permute-start | bytes 786440 | tf_op jit(solution)/shard_map/ppermute | solution.py:140
  21.0 11.4 %collective-permute-start.2 = (bf16[2,32,2048]{2,1,0:T(8,128)(2,1)S(1)}, bf16[2,32,2048]{2,1,0:T(8,128)(2,1)S(1)}, u32[]{:S(2)}, u32[]{:S(2)}) collective-permute-start(bf16[2,32,2048]{2,1,0:T(8,128)(2,1)S(1)} %pad_maximum_fusion.1), channel_id=1, source_target_pairs={{0,256},{128,1},{256,257},{384,0},{1,384},{129,129},{257,385},{385... | collective-permute-start | bytes 786440 | tf_op jit(solution)/shard_map/ppermute | solution.py:140
  24.0 43.2 %all-to-all-start = ((bf16[8,48,1152]{2,1,0:T(8,128)(2,1)}), bf16[8,48,1152]{2,1,0:T(8,128)(2,1)S(1)}, u32[]{:S(2)}, u32[]{:S(2)}) async-start(bf16[8,48,1152]{2,1,0:T(8,128)(2,1)} %pad_maximum_fusion), calls=%async_computation | async-start | bytes 1769472 | tf_op jit(solution)/shard_map/all_to_all | solution.py:212
  32.5 38.4 %copy-start.2 = (bf16[4,32,2048]{2,1,0:T(8,128)(2,1)}, bf16[4,32,2048]{2,1,0:T(8,128)(2,1)S(1)}, u32[]{:S(2)}) copy-start(bf16[4,32,2048]{2,1,0:T(8,128)(2,1)S(1)} %constant_dynamic-update-slice_fusion.rest_0_) | copy-start | bytes 1572868
  32.5 6.6 %collective-permute-start.8 = (bf16[4,32,2048]{2,1,0:T(8,128)(2,1)S(1)}, bf16[4,32,2048]{2,1,0:T(8,128)(2,1)S(1)}, u32[]{:S(2)}, u32[]{:S(2)}) collective-permute-start(bf16[4,32,2048]{2,1,0:T(8,128)(2,1)S(1)} %constant_dynamic-update-slice_fusion.rest_0_), channel_id=1, source_target_pairs={{0,8},{8,0},{1,9},{9,1},{2,10},{10,2},{3,11},{11,3},{4,12},{12,4},... | collective-permute-start | bytes 1572872 | tf_op jit(solution)/shard_map/ppermute | solution.py:50
  35.0 10.3 %collective-permute-start.3 = (bf16[4,32,2048]{2,1,0:T(8,128)(2,1)S(1)}, bf16[4,32,2048]{2,1,0:T(8,128)(2,1)S(1)}, u32[]{:S(2)}, u32[]{:S(2)}) collective-permute-start(bf16[4,32,2048]{2,1,0:T(8,128)(2,1)S(1)} %constant_dynamic-update-slice_fusion.rest_0_), channel_id=1, source_target_pairs={{0,16},{16,32},{32,48},{48,64},{64,80},{80,96},{96,112},{112,0},{8... | collective-permute-start | bytes 1572872 | tf_op jit(solution)/shard_map/ppermute | solution.py:146
  39.2 11.8 %collective-permute-start.9 = (bf16[4,32,2048]{2,1,0:T(8,128)(2,1)S(1)}, bf16[4,32,2048]{2,1,0:T(8,128)(2,1)}, u32[]{:S(2)}, u32[]{:S(2)}) collective-permute-start(bf16[4,32,2048]{2,1,0:T(8,128)(2,1)S(1)} %collective-permute-done.8.rest_1_), channel_id=1, source_target_pairs={{0,16},{16,32},{32,48},{48,64},{64,80},{80,96},{96,112},{112,0},{8... | collective-permute-start | bytes 1572872 | tf_op jit(solution)/shard_map/ppermute | solution.py:146
  45.3 13.9 %collective-permute-start.4 = (bf16[4,32,2048]{2,1,0:T(8,128)(2,1)S(1)}, bf16[4,32,2048]{2,1,0:T(8,128)(2,1)}, u32[]{:S(2)}, u32[]{:S(2)}) collective-permute-start(bf16[4,32,2048]{2,1,0:T(8,128)(2,1)S(1)} %collective-permute-done.3.rest_2_), channel_id=1, source_target_pairs={{0,16},{16,32},{32,48},{48,64},{64,80},{80,96},{96,112},{112,0},{8... | collective-permute-start | bytes 1572872 | tf_op jit(solution)/shard_map/ppermute | solution.py:146
  50.9 16.8 %collective-permute-start.10 = (bf16[4,32,2048]{2,1,0:T(8,128)(2,1)}, bf16[4,32,2048]{2,1,0:T(8,128)(2,1)}, u32[]{:S(2)}, u32[]{:S(2)}) collective-permute-start(bf16[4,32,2048]{2,1,0:T(8,128)(2,1)} %collective-permute-done.9.rest_4_), channel_id=1, source_target_pairs={{0,16},{16,32},{32,48},{48,64},{64,80},{80,96},{96,112},{112,0},{8... | collective-permute-start | bytes 1572872 | tf_op jit(solution)/shard_map/ppermute | solution.py:146
  57.2 32.5 %collective-permute-start.13 = (bf16[4,32,2048]{2,1,0:T(8,128)(2,1)S(1)}, bf16[4,32,2048]{2,1,0:T(8,128)(2,1)}, u32[]{:S(2)}, u32[]{:S(2)}) collective-permute-start(bf16[4,32,2048]{2,1,0:T(8,128)(2,1)S(1)} %collective-permute-done.3.rest_2_), channel_id=1, source_target_pairs={{0,8},{8,0},{1,9},{9,1},{2,10},{10,2},{3,11},{11,3},{4,12},{12,4},... | collective-permute-start | bytes 1572872 | tf_op jit(solution)/shard_map/ppermute | solution.py:50
  59.1 12.3 %collective-permute-start.5 = (bf16[4,32,2048]{2,1,0:T(8,128)(2,1)}, bf16[4,32,2048]{2,1,0:T(8,128)(2,1)}, u32[]{:S(2)}, u32[]{:S(2)}) collective-permute-start(bf16[4,32,2048]{2,1,0:T(8,128)(2,1)} %collective-permute-done.4.rest_6_), channel_id=1, source_target_pairs={{0,16},{16,32},{32,48},{48,64},{64,80},{80,96},{96,112},{112,0},{8... | collective-permute-start | bytes 1572872 | tf_op jit(solution)/shard_map/ppermute | solution.py:146
  62.9 29.3 %collective-permute-start.15 = (bf16[4,32,2048]{2,1,0:T(8,128)(2,1)}, bf16[4,32,2048]{2,1,0:T(8,128)(2,1)}, u32[]{:S(2)}, u32[]{:S(2)}) collective-permute-start(bf16[4,32,2048]{2,1,0:T(8,128)(2,1)} %collective-permute-done.4.rest_6_), channel_id=1, source_target_pairs={{0,8},{8,0},{1,9},{9,1},{2,10},{10,2},{3,11},{11,3},{4,12},{12,4},... | collective-permute-start | bytes 1572872 | tf_op jit(solution)/shard_map/ppermute | solution.py:50
  64.8 27.3 %collective-permute-start.14 = (bf16[4,32,2048]{2,1,0:T(8,128)(2,1)}, bf16[4,32,2048]{2,1,0:T(8,128)(2,1)}, u32[]{:S(2)}, u32[]{:S(2)}) collective-permute-start(bf16[4,32,2048]{2,1,0:T(8,128)(2,1)} %collective-permute-done.9.rest_4_), channel_id=1, source_target_pairs={{0,8},{8,0},{1,9},{9,1},{2,10},{10,2},{3,11},{11,3},{4,12},{12,4},... | collective-permute-start | bytes 1572872 | tf_op jit(solution)/shard_map/ppermute | solution.py:50
  67.8 10.5 %collective-permute-start.11 = (bf16[4,32,2048]{2,1,0:T(8,128)(2,1)}, bf16[4,32,2048]{2,1,0:T(8,128)(2,1)}, u32[]{:S(2)}, u32[]{:S(2)}) collective-permute-start(bf16[4,32,2048]{2,1,0:T(8,128)(2,1)} %collective-permute-done.10.rest_8_), channel_id=1, source_target_pairs={{0,16},{16,32},{32,48},{48,64},{64,80},{80,96},{96,112},{112,0},{8... | collective-permute-start | bytes 1572872 | tf_op jit(solution)/shard_map/ppermute | solution.py:146
  71.4 12.4 %collective-permute-start.6 = (bf16[4,32,2048]{2,1,0:T(8,128)(2,1)}, bf16[4,32,2048]{2,1,0:T(8,128)(2,1)S(1)}, u32[]{:S(2)}, u32[]{:S(2)}) collective-permute-start(bf16[4,32,2048]{2,1,0:T(8,128)(2,1)} %collective-permute-done.5.rest_10_), channel_id=1, source_target_pairs={{0,16},{16,32},{32,48},{48,64},{64,80},{80,96},{96,112},{112,0},{8... | collective-permute-start | bytes 1572872 | tf_op jit(solution)/shard_map/ppermute | solution.py:146
  78.3 9.5 %collective-permute-start.12 = (bf16[4,32,2048]{2,1,0:T(8,128)(2,1)}, bf16[4,32,2048]{2,1,0:T(8,128)(2,1)S(1)}, u32[]{:S(2)}, u32[]{:S(2)}) collective-permute-start(bf16[4,32,2048]{2,1,0:T(8,128)(2,1)} %collective-permute-done.11.rest_12_), channel_id=1, source_target_pairs={{0,8},{8,0},{1,9},{9,1},{2,10},{10,2},{3,11},{11,3},{4,12},{12,4},... | collective-permute-start | bytes 1572872 | tf_op jit(solution)/shard_map/ppermute | solution.py:50
  83.8 8.4 %collective-permute-start.17 = (bf16[4,32,2048]{2,1,0:T(8,128)(2,1)}, bf16[4,32,2048]{2,1,0:T(8,128)(2,1)}, u32[]{:S(2)}, u32[]{:S(2)}) collective-permute-start(bf16[4,32,2048]{2,1,0:T(8,128)(2,1)} %collective-permute-done.5.rest_10_), channel_id=1, source_target_pairs={{0,8},{8,0},{1,9},{9,1},{2,10},{10,2},{3,11},{11,3},{4,12},{12,4},... | collective-permute-start | bytes 1572872 | tf_op jit(solution)/shard_map/ppermute | solution.py:50
  87.8 4.4 %collective-permute-start.16 = (bf16[4,32,2048]{2,1,0:T(8,128)(2,1)}, bf16[4,32,2048]{2,1,0:T(8,128)(2,1)}, u32[]{:S(2)}, u32[]{:S(2)}) collective-permute-start(bf16[4,32,2048]{2,1,0:T(8,128)(2,1)} %collective-permute-done.10.rest_8_), channel_id=1, source_target_pairs={{0,8},{8,0},{1,9},{9,1},{2,10},{10,2},{3,11},{11,3},{4,12},{12,4},... | collective-permute-start | bytes 1572872 | tf_op jit(solution)/shard_map/ppermute | solution.py:50
  89.7 3.9 %collective-permute-start.18 = (bf16[4,32,2048]{2,1,0:T(8,128)(2,1)S(1)}, bf16[4,32,2048]{2,1,0:T(8,128)(2,1)S(1)}, u32[]{:S(2)}, u32[]{:S(2)}) collective-permute-start(bf16[4,32,2048]{2,1,0:T(8,128)(2,1)S(1)} %collective-permute-done.6.rest_14_), channel_id=1, source_target_pairs={{0,8},{8,0},{1,9},{9,1},{2,10},{10,2},{3,11},{11,3},{4,12},{12,4},... | collective-permute-start | bytes 1572872 | tf_op jit(solution)/shard_map/ppermute | solution.py:50
  129.2 28.6 %all-to-all-start.2 = ((f32[64,8,128]{2,1,0:T(8,128)}), f32[64,8,128]{2,1,0:T(8,128)S(1)}, u32[]{:S(2)}, u32[]{:S(2)}) async-start(f32[64,8,128]{2,1,0:T(8,128)} %broadcast_in_dim.35), calls=%async_computation.2 | async-start | bytes 524288 | tf_op jit(solution)/shard_map/all_to_all | solution.py:160
  158.7 16.2 %all-to-all-start.3 = ((bf16[8,48,1024]{2,1,0:T(8,128)(2,1)}), bf16[8,48,1024]{2,1,0:T(8,128)(2,1)S(1)}, u32[]{:S(2)}, u32[]{:S(2)}) async-start(bf16[8,48,1024]{2,1,0:T(8,128)(2,1)} %broadcast_dynamic-update-slice_fusion), calls=%async_computation.3 | async-start | bytes 1572864 | tf_op jit(solution)/shard_map/all_to_all | solution.py:296
  162.7 5.4 %collective-permute-start.19 = (f32[4,1024]{1,0:T(4,128)S(1)}, f32[4,1024]{1,0:T(4,128)S(1)}, u32[]{:S(2)}, u32[]{:S(2)}) collective-permute-start(f32[4,1024]{1,0:T(4,128)S(1)} %constant_dynamic-slice_fusion.1), channel_id=1, source_target_pairs={{8,0},{16,8},{24,16},{32,24},{40,32},{48,40},{56,48},{64,56},{72,6... | collective-permute-start | bytes 49160 | tf_op jit(solution)/shard_map/ppermute | solution.py:312
  (10 other events, 168.9 us)
